TPU v7x, 256 devices: a whole 4x4x8 slice. The times are simulated.
256 devices in a mesh: dp: 16 (over x, z_lo), width: 8 (over y, core), grid: 2 (over z_hi).
Axes of the slice: x: 4, y: 4, z: 8 (z_hi: 2, z_lo: 4; z = z_hi * 4 + z_lo), core: 2. Of those that a mesh axis runs over, the one named last changes fastest.
Arguments:
- train_acts: bfloat16 [12288, 16384], P(('dp', 'grid'), 'width'), may hold values from -6 to 6
- train_grads: bfloat16 [12288, 16384], P(('dp', 'grid'), 'width'), may hold values from -6 to 6
- query_acts: bfloat16 [512, 16384], P('dp', 'width'), may hold values from -6 to 6
- query_grads: bfloat16 [512, 16384], P('dp', 'width'), may hold values from -6 to 6
- act_inverse: bfloat16 [16384, 16384], P(('dp', 'grid'), 'width'), may hold values from -0.046875 to 0.046875
- grad_inverse: bfloat16 [16384, 16384], P(('dp', 'grid'), 'width'), may hold values from -0.046875 to 0.046875
- query_slot: int32 [16], replicated, may hold values from 0 to 15, each once
- resident: int32 [12288], P(('dp', 'grid')), may hold values 0 or 1
Outputs:
- scores: float32 [12288, 16], P(('dp', 'grid'), 'width')
All inputs are finite; a program needn't handle non-finite values. No bound on the sum of `resident` on one device may be relied on, other than what follows from the above.
Results may differ from a plain program's by a relative error of at most 0.0041.
Values may be sent and summed in bfloat16 or wider, within the bound.
No kernel may reach another device: no remote copies, remote signals or barrier semaphores. Data moves between devices by JAX's collectives and lax.ppermute only.
A program may use at most 64 MiB of HBM per device.

v0:
```python
import functools
import itertools
import math

import jax
import jax.numpy as jnp
from jax import lax
from jax.experimental import pallas as pl
from jax.experimental.pallas import tpu as pltpu
from jax.sharding import PartitionSpec as P


D = 16384
QTOK = 32
AXES = ("dp", "width", "grid")
F32 = jnp.float32
BF16 = jnp.bfloat16


def device(x, y, z, c):
    x, y, z, c = x % 4, y % 4, z % 8, c % 2
    return ((4 * x + z % 4) * 8 + 2 * y + c) * 2 + z // 4


def move(target):
    return [
        (device(x, y, z, c), device(*target(x, y, z, c)))
        for x, y, z, c in itertools.product(range(4), range(4), range(8), range(2))
    ]


def along_x(value, step):
    return lax.ppermute(value, AXES, move(lambda x, y, z, c: (x + step, y, z, c)))


def along_y(value, step):
    return lax.ppermute(value, AXES, move(lambda x, y, z, c: (x, y + step, z, c)))


def along_z(value, step):
    return lax.ppermute(value, AXES, move(lambda x, y, z, c: (x, y, z + step, c)))


def other_core(value):
    return lax.ppermute(value, AXES, move(lambda x, y, z, c: (x, y, z, c + 1)))


def far_z(value):
    return lax.ppermute(value, AXES, move(lambda x, y, z, c: (x, y, z + 2 - 4 * c, c)))


def to_owner(value, step):
    def target(x, y, z, c):
        high, middle, low = z // 4, (z // 2) % 2, z % 2
        return (x + y, x, 4 * high + 2 * c + low + step, middle)

    return lax.ppermute(value, AXES, move(target))


def vmem():
    return pl.BlockSpec(memory_space=pltpu.VMEM)


def smem():
    return pl.BlockSpec(memory_space=pltpu.SMEM)


def anywhere():
    return pl.BlockSpec(memory_space=pl.ANY)


def chunk_row(slot_pair, y, c):
    core = lax.rem(slot_pair, 2)
    ahead = lax.rem(lax.div(slot_pair, 2) - y + 4, 4)
    return jnp.where(core == c, 256, 0) + ahead * 64


def nt_dot(a, b):
    return lax.dot_general(a, b, (((1,), (1,)), ((), ())), preferred_element_type=F32)


X_FROM = (0, 2, -1, 1)


def z_from(c):
    return (0, jnp.where(c == 0, -2, 2), -1, 1)


def tiles(out, rows, inv, first):
    def tile(t, _):
        at = pl.multiple_of(256 * t, 256)
        out[:, pl.ds(at, 256)] = nt_dot(rows[first : first + 256, :], inv[pl.ds(at, 256), :])
        return 0

    lax.fori_loop(0, inv.shape[0] // 256, tile, 0)


def piece_offsets(z_first, c):
    for second in range(4):
        for first in range(4):
            if z_first:
                yield second, first, X_FROM[second], z_from(c)[first]
            else:
                yield second, first, X_FROM[first], z_from(c)[second]


def precondition_kernel(z_first, place, slots, *refs):
    bundles, (inv, send, rows, sem) = refs[:4], refs[4:]
    x, y, z, c = place[0], place[1], place[2], place[3]
    copies = []
    for second, first, dx, dz in piece_offsets(z_first, c):
        query = lax.rem(x + dx + 4, 4) * 4 + lax.rem(z + dz + 8, 4)
        slot = slots[query]
        row = chunk_row(lax.div(slot, 2), y, c) + 32 * lax.rem(slot, 2)
        target = rows.at[pl.ds(pl.multiple_of(row, 32), 32), :]
        copy = pltpu.make_async_copy(bundles[second].at[first], target, sem)
        copy.start()
        copies.append(copy)
    for copy in copies:
        copy.wait()
    tiles(send, rows, inv, 0)


def keep_kernel(rows, right, keep):
    tiles(keep, rows, right, 256)


def estimate():
    return pl.CostEstimate(flops=2**29, bytes_accessed=2**20, transcendentals=0)


def precondition(place, slots, bundles, inv, z_first):
    return pl.pallas_call(
        functools.partial(precondition_kernel, z_first),
        out_shape=(
            jax.ShapeDtypeStruct((256, 512), F32),
            jax.ShapeDtypeStruct((512, 2048), BF16),
        ),
        in_specs=[smem(), smem()] + [anywhere()] * 4 + [vmem()],
        out_specs=(vmem(),) * 2,
        scratch_shapes=[pltpu.SemaphoreType.DMA(())],
        compiler_params=limit(8),
        cost_estimate=estimate(),
        name="precondition",
    )(place, slots, *bundles, inv)


def kept(rows, right):
    return pl.pallas_call(
        keep_kernel if right.shape[0] % 256 == 0 else project_keep_kernel,
        out_shape=jax.ShapeDtypeStruct((256, right.shape[0]), F32),
        in_specs=[vmem()] * 2,
        out_specs=vmem(),
        compiler_params=limit(8),
        cost_estimate=estimate(),
    )(rows, right)


def stack_kernel(*refs):
    sources, (out, sems) = refs[:-2], refs[-2:]
    copies = [
        pltpu.make_async_copy(source, out.at[i], sems.at[i]) for i, source in enumerate(sources)
    ]
    for copy in copies:
        copy.start()
    for copy in copies:
        copy.wait()


def stack(*arrays):
    count = len(arrays)
    return pl.pallas_call(
        stack_kernel,
        out_shape=jax.ShapeDtypeStruct((count,) + arrays[0].shape, arrays[0].dtype),
        in_specs=[anywhere()] * count,
        out_specs=vmem(),
        scratch_shapes=[pltpu.SemaphoreType.DMA((count,))],
        compiler_params=limit(2),
        name="stack",
    )(*arrays)


def limit(mib):
    return pltpu.CompilerParams(vmem_limit_bytes=mib << 20)


def split_kernel(keep_a, keep_g, got_a, got_g, *outs):
    for step, out in enumerate(outs):
        rows = slice(64 * step, 64 * step + 64)
        out[0] = keep_a[rows, :] + got_a[rows, :]
        out[1] = keep_g[rows, :] + got_g[rows, :]


def split(keep, got):
    shape = jax.ShapeDtypeStruct((2, 64, keep[0].shape[-1]), F32)
    return pl.pallas_call(
        split_kernel,
        out_shape=(shape,) * 4,
        in_specs=[vmem()] * 4,
        out_specs=(vmem(),) * 4,
        compiler_params=limit(6),
        name="split",
    )(*keep, *got)


def factor_kernel(p0, p1, p2, p3, out):
    out[...] = ((p0[...] + p1[...]) + (p2[...] + p3[...])).astype(BF16)


def factor_sum(parts):
    return pl.pallas_call(
        factor_kernel,
        out_shape=jax.ShapeDtypeStruct((2, 64, 512), BF16),
        in_specs=[vmem()] * 4,
        out_specs=vmem(),
        compiler_params=limit(4),
        name="factor_sum",
    )(*parts)


def project_kernel(z_first, place, *refs):
    bundles, (tok, send, factor, sem) = refs[:4], refs[4:]
    x, y, c = place[0], place[1], place[3]
    ring = place[4]
    copies = []
    for second, first, dx, dz in piece_offsets(z_first, c):
        for high in range(2):
            px = lax.rem(x + dx - y + 8, 4)
            pz = lax.rem(ring + dz + 4 * high + 8, 8)
            row = chunk_row(2 * px + lax.rem(lax.div(pz, 2), 2), y, c)
            column = (2 * lax.rem(pz, 2) + lax.div(pz, 4)) * 512
            target = factor.at[
                pl.ds(pl.multiple_of(row, 64), 64), pl.ds(pl.multiple_of(column, 512), 512)
            ]
            copy = pltpu.make_async_copy(bundles[second].at[first, high], target, sem)
            copy.start()
            copies.append(copy)
    for copy in copies:
        copy.wait()
    send[...] = nt_dot(factor[:256, :], tok[...])


def project_keep_kernel(factor, tok, keep):
    keep[...] = nt_dot(factor[256:, :], tok[...])


def project(place, bundles, tok, z_first):
    return pl.pallas_call(
        functools.partial(project_kernel, z_first),
        out_shape=(
            jax.ShapeDtypeStruct((256, tok.shape[0]), F32),
            jax.ShapeDtypeStruct((512, 2048), BF16),
        ),
        in_specs=[smem()] + [anywhere()] * 4 + [vmem()],
        out_specs=(vmem(),) * 2,
        scratch_shapes=[pltpu.SemaphoreType.DMA(())],
        compiler_params=limit(8),
        cost_estimate=estimate(),
        name="project",
    )(place, *bundles, tok)


def score_kernel(p0, p1, p2, p3, resident, out):
    acts = (p0[0] + p1[0]) + (p2[0] + p3[0])
    grads = (p0[1] + p1[1]) + (p2[1] + p3[1])
    product = acts * grads
    scale = 1.0 / (D * math.sqrt(QTOK))
    here = resident[...].astype(F32)
    for query in range(2):
        total = jnp.sum(product[QTOK * query : QTOK * query + QTOK], axis=0, keepdims=True)
        out[query : query + 1, :] = total * scale * here


def score(parts, resident):
    tokens = resident.shape[-1]
    return pl.pallas_call(
        score_kernel,
        out_shape=jax.ShapeDtypeStruct((2, tokens), F32),
        in_specs=[vmem()] * 5,
        out_specs=vmem(),
        compiler_params=limit(6),
        name="score",
    )(*parts, resident)


def local(
    train_acts,
    train_grads,
    query_acts,
    query_grads,
    act_inverse,
    grad_inverse,
    query_slot,
    resident,
):
    dp, width, grid = (lax.axis_index(name) for name in AXES)
    place = jnp.stack([dp // 4, width // 2, dp % 4, width % 2, 4 * grid + dp % 4])
    place, query_slot, query_acts = lax.optimization_barrier((place, query_slot, query_acts))

    def x_others(value):
        out = []
        for step in (2, 1, -1):
            out.append(along_x(value, step))
        return out

    def z_others(value):
        out = [far_z(value)]
        for step in (1, -1):
            out.append(along_z(value, step))
        return out

    def gather(acts, grads):
        ax, gz = x_others(acts), z_others(grads)
        ax, gz = stack(acts, *ax), stack(grads, *gz)
        gzx = [gz] + x_others(gz)
        axz = [ax] + z_others(ax)
        return axz, gzx

    bundles = gather(query_acts, query_grads)
    halves = []
    for array, inv in enumerate((act_inverse, grad_inverse)):
        send, rows = precondition(place, query_slot, bundles[array], inv, array == 1)
        got = other_core(send)
        halves.append((kept(rows, inv), got))
    parts = split(*zip(*halves))
    moved = [parts[0]]
    for step in (2, 1, 3):
        moved.append(along_y(parts[step], step))
    factor = factor_sum(moved)
    owner_4 = to_owner(factor, 4)
    owner_0 = to_owner(factor, 0)
    bundles = gather(*(jnp.stack([owner_0[array], owner_4[array]]) for array in range(2)))
    halves = []
    for array, tok in enumerate((train_acts, train_grads)):
        send, rows = project(place, bundles[array], tok, array == 1)
        got = other_core(send)
        halves.append((kept(rows, tok), got))
    parts = split(*zip(*halves))
    moved = [parts[0]]
    for step in (2, 1, 3):
        moved.append(along_y(parts[step], step))
    return score(moved, resident.reshape(1, -1)).T


def solution(mesh):
    return jax.shard_map(
        local,
        mesh=mesh,
        in_specs=(
            P(("dp", "grid"), "width"),
            P(("dp", "grid"), "width"),
            P("dp", "width"),
            P("dp", "width"),
            P(("dp", "grid"), "width"),
            P(("dp", "grid"), "width"),
            P(),
            P(("dp", "grid")),
        ),
        out_specs=P(("dp", "grid"), "width"),
        check_vma=False,
    )
```

profile of v0, /device:TPU:2, one launch (start us, length us, event | category | flops | bytes accessed | tf_op | source)
XLA Modules:
  0.0 177.9 jit_solution(12588794292921789313)
XLA Ops:
  0.0 3.3 %collective-permute-start.6 = (bf16[32,2048]{1,0:T(8,128)(2,1)}, bf16[32,2048]{1,0:T(8,128)(2,1)S(1)}, u32[]{:S(2)}, u32[]{:S(2)}) collective-permute-start(bf16[32,2048]{1,0:T(8,128)(2,1)} %refs_0_.2), channel_id=1, source_target_pairs={{0,32},{2,35},{16,48},{18,51},{32,1},{34,2},{48,17},{50,18},{1,33}... | collective-permute-start | bytes 393224 | tf_op jit(solution)/shard_map/ppermute | solution.py:49
  3.3 1.9 %collective-permute-start.7 = (bf16[32,2048]{1,0:T(8,128)(2,1)}, bf16[32,2048]{1,0:T(8,128)(2,1)S(1)}, u32[]{:S(2)}, u32[]{:S(2)}) collective-permute-start(bf16[32,2048]{1,0:T(8,128)(2,1)} %refs_0_.2), channel_id=1, source_target_pairs={{0,16},{2,18},{16,32},{18,34},{32,48},{34,50},{48,1},{50,3},{1,17}... | collective-permute-start | bytes 393224 | tf_op jit(solution)/shard_map/ppermute | solution.py:41
  5.2 1.3 collective-permute-start.8
  6.5 3.4 %collective-permute-done.6.refs_1_ = bf16[32,2048]{1,0:T(8,128)(2,1)S(1)} collective-permute-done((bf16[32,2048]{1,0:T(8,128)(2,1)}, bf16[32,2048]{1,0:T(8,128)(2,1)S(1)}, u32[]{:S(2)}, u32[]{:S(2)}) %collective-permute-start.6) | collective-permute-done | bytes 131104 | tf_op jit(solution)/shard_map/ppermute | solution.py:49
  9.9 3.3 %collective-permute-done.7.refs_2_ = bf16[32,2048]{1,0:T(8,128)(2,1)S(1)} collective-permute-done((bf16[32,2048]{1,0:T(8,128)(2,1)}, bf16[32,2048]{1,0:T(8,128)(2,1)S(1)}, u32[]{:S(2)}, u32[]{:S(2)}) %collective-permute-start.7) | collective-permute-done | bytes 131104 | tf_op jit(solution)/shard_map/ppermute | solution.py:41
  14.8 1.6 collective-permute-start.10
  16.5 1.1 collective-permute-start
  18.5 1.3 collective-permute-start.2
  19.8 3.2 %collective-permute-start.11 = (bf16[4,32,2048]{2,1,0:T(8,128)(2,1)S(1)}, bf16[4,32,2048]{2,1,0:T(8,128)(2,1)S(1)}, u32[]{:S(2)}, u32[]{:S(2)}) collective-permute-start(bf16[4,32,2048]{2,1,0:T(8,128)(2,1)S(1)} %stack.37.refs_0_), channel_id=1, source_target_pairs={{0,192},{2,194},{16,208},{18,210},{32,224},{34,226},{48,240},{50,2... | collective-permute-start | bytes 1572872 | tf_op jit(solution)/shard_map/ppermute | solution.py:33
  23.0 1.6 collective-permute-done.refs_1_
  25.5 8.4 %collective-permute-done.1.refs_2_ = bf16[32,2048]{1,0:T(8,128)(2,1)S(1)} collective-permute-done((bf16[32,2048]{1,0:T(8,128)(2,1)}, bf16[32,2048]{1,0:T(8,128)(2,1)S(1)}, u32[]{:S(2)}, u32[]{:S(2)}) %collective-permute-start.1) | collective-permute-done | bytes 131104 | tf_op jit(solution)/shard_map/ppermute | solution.py:33
  35.5 1.2 collective-permute-start.3
  36.7 2.2 %collective-permute-start.4 = (bf16[4,32,2048]{2,1,0:T(8,128)(2,1)S(1)}, bf16[4,32,2048]{2,1,0:T(8,128)(2,1)S(1)}, u32[]{:S(2)}, u32[]{:S(2)}) collective-permute-start(bf16[4,32,2048]{2,1,0:T(8,128)(2,1)S(1)} %stack.36.refs_0_), channel_id=1, source_target_pairs={{0,16},{2,18},{16,32},{18,34},{32,48},{34,50},{48,1},{50,3},{1,17}... | collective-permute-start | bytes 1572872 | tf_op jit(solution)/shard_map/ppermute | solution.py:41
  38.9 1.0 collective-permute-start.5
  40.0 8.4 %collective-permute-done.9.refs_1_ = bf16[4,32,2048]{2,1,0:T(8,128)(2,1)S(1)} collective-permute-done((bf16[4,32,2048]{2,1,0:T(8,128)(2,1)S(1)}, bf16[4,32,2048]{2,1,0:T(8,128)(2,1)S(1)}, u32[]{:S(2)}, u32[]{:S(2)}) %collective-permute-start.9) | collective-permute-done | bytes 524320 | tf_op jit(solution)/shard_map/ppermute | solution.py:33
  49.0 4.7 %precondition.3 = (f32[256,512]{1,0:T(8,128)S(1)}, bf16[512,2048]{1,0:T(8,128)(2,1)S(1)}) custom-call(s32[5]{0:T(128)S(1)} %stack.33.place, s32[16]{0:T(128)S(1)} %copy-done.6, bf16[4,32,2048]{2,1,0:T(8,128)(2,1)S(1)} %stack.37.refs_0_, bf16[4,32,2048]{2,1,0:T(8,128)(2,1)S(1)} %collective-permute-done.9.refs_1_, ...), custom_call_target="tpu_custom_call" | custom-call | flops 536870912 | bytes 1048576 | tf_op jit(solution)/shard_map/precondition/pallas_call | solution.py:133
  53.9 3.5 %collective-permute-done.3.refs_1_ = bf16[4,32,2048]{2,1,0:T(8,128)(2,1)S(1)} collective-permute-done((bf16[4,32,2048]{2,1,0:T(8,128)(2,1)S(1)}, bf16[4,32,2048]{2,1,0:T(8,128)(2,1)S(1)}, u32[]{:S(2)}, u32[]{:S(2)}) %collective-permute-start.3) | collective-permute-done | bytes 524320 | tf_op jit(solution)/shard_map/ppermute | solution.py:49
  57.3 5.5 %collective-permute-done.4.refs_2_ = bf16[4,32,2048]{2,1,0:T(8,128)(2,1)S(1)} collective-permute-done((bf16[4,32,2048]{2,1,0:T(8,128)(2,1)S(1)}, bf16[4,32,2048]{2,1,0:T(8,128)(2,1)S(1)}, u32[]{:S(2)}, u32[]{:S(2)}) %collective-permute-start.4) | collective-permute-done | bytes 524320 | tf_op jit(solution)/shard_map/ppermute | solution.py:41
  62.8 4.7 %precondition.2 = (f32[256,512]{1,0:T(8,128)S(1)}, bf16[512,2048]{1,0:T(8,128)(2,1)S(1)}) custom-call(s32[5]{0:T(128)S(1)} %stack.33.place, s32[16]{0:T(128)S(1)} %copy-done.6, bf16[4,32,2048]{2,1,0:T(8,128)(2,1)S(1)} %stack.36.refs_0_, bf16[4,32,2048]{2,1,0:T(8,128)(2,1)S(1)} %collective-permute-done.3.refs_1_, ...), custom_call_target="tpu_custom_call" | custom-call | flops 536870912 | bytes 1048576 | tf_op jit(solution)/shard_map/precondition/pallas_call | solution.py:133
  69.9 3.3 %collective-permute-start.14 = (f32[2,64,512]{2,1,0:T(8,128)S(1)}, f32[2,64,512]{2,1,0:T(8,128)S(1)}, u32[]{:S(2)}, u32[]{:S(2)}) collective-permute-start(f32[2,64,512]{2,1,0:T(8,128)S(1)} %get-tuple-element.32), channel_id=1, source_target_pairs={{0,8},{2,10},{16,24},{18,26},{32,40},{34,42},{48,56},{50,58},{1,9}... | collective-permute-start | bytes 786440 | tf_op jit(solution)/shard_map/ppermute | solution.py:37
  73.8 2.6 %collective-permute-start.16 = (f32[2,64,512]{2,1,0:T(8,128)S(1)}, f32[2,64,512]{2,1,0:T(8,128)S(1)}, u32[]{:S(2)}, u32[]{:S(2)}) collective-permute-start(f32[2,64,512]{2,1,0:T(8,128)S(1)} %get-tuple-element.34), channel_id=1, source_target_pairs={{0,12},{2,14},{16,28},{18,30},{32,44},{34,46},{48,60},{50,62},{1,1... | collective-permute-start | bytes 786440 | tf_op jit(solution)/shard_map/ppermute | solution.py:37
  76.4 4.3 %collective-permute-done.14.p1 = f32[2,64,512]{2,1,0:T(8,128)S(1)} collective-permute-done((f32[2,64,512]{2,1,0:T(8,128)S(1)}, f32[2,64,512]{2,1,0:T(8,128)S(1)}, u32[]{:S(2)}, u32[]{:S(2)}) %collective-permute-start.14) | collective-permute-done | bytes 262176 | tf_op jit(solution)/shard_map/ppermute | solution.py:37
  80.7 5.1 %collective-permute-done.15.p2 = f32[2,64,512]{2,1,0:T(8,128)S(1)} collective-permute-done((f32[2,64,512]{2,1,0:T(8,128)S(1)}, f32[2,64,512]{2,1,0:T(8,128)S(1)}, u32[]{:S(2)}, u32[]{:S(2)}) %collective-permute-start.15) | collective-permute-done | bytes 262176 | tf_op jit(solution)/shard_map/ppermute | solution.py:37
  86.3 3.4 %collective-permute-start.17 = (bf16[2,64,512]{2,1,0:T(8,128)(2,1)S(1)}, bf16[2,64,512]{2,1,0:T(8,128)(2,1)S(1)}, u32[]{:S(2)}, u32[]{:S(2)}) collective-permute-start(bf16[2,64,512]{2,1,0:T(8,128)(2,1)S(1)} %factor_sum.1), channel_id=1, source_target_pairs={{0,0},{2,32},{16,16},{18,48},{32,2},{34,34},{48,18},{50,50},{1,1},... | collective-permute-start | bytes 393224 | tf_op jit(solution)/shard_map/ppermute | solution.py:57
  89.7 1.3 collective-permute-start.18
  91.0 3.2 %collective-permute-done.17 = bf16[2,64,512]{2,1,0:T(8,128)(2,1)S(1)} collective-permute-done((bf16[2,64,512]{2,1,0:T(8,128)(2,1)S(1)}, bf16[2,64,512]{2,1,0:T(8,128)(2,1)S(1)}, u32[]{:S(2)}, u32[]{:S(2)}) %collective-permute-start.17) | collective-permute-done | bytes 131104 | tf_op jit(solution)/shard_map/ppermute | solution.py:57
  94.2 6.3 %collective-permute-done.18 = bf16[2,64,512]{2,1,0:T(8,128)(2,1)S(1)} collective-permute-done((bf16[2,64,512]{2,1,0:T(8,128)(2,1)S(1)}, bf16[2,64,512]{2,1,0:T(8,128)(2,1)S(1)}, u32[]{:S(2)}, u32[]{:S(2)}) %collective-permute-start.18) | collective-permute-done | bytes 131104 | tf_op jit(solution)/shard_map/ppermute | solution.py:57
  100.5 2.3 %collective-permute-start.25 = (bf16[2,64,512]{2,1,0:T(8,128)(2,1)S(1)}, bf16[2,64,512]{2,1,0:T(8,128)(2,1)S(1)}, u32[]{:S(2)}, u32[]{:S(2)}) collective-permute-start(bf16[2,64,512]{2,1,0:T(8,128)(2,1)S(1)} %pad_maximum_fusion.1.refs_0_), channel_id=1, source_target_pairs={{0,32},{2,35},{16,48},{18,51},{32,1},{34,2},{48,17},{50,18},{1,33}... | collective-permute-start | bytes 393224 | tf_op jit(solution)/shard_map/ppermute | solution.py:49
  102.8 3.2 %collective-permute-start.27 = (bf16[2,64,512]{2,1,0:T(8,128)(2,1)S(1)}, bf16[2,64,512]{2,1,0:T(8,128)(2,1)S(1)}, u32[]{:S(2)}, u32[]{:S(2)}) collective-permute-start(bf16[2,64,512]{2,1,0:T(8,128)(2,1)S(1)} %pad_maximum_fusion.1.refs_0_), channel_id=1, source_target_pairs={{0,49},{2,51},{16,0},{18,2},{32,16},{34,18},{48,32},{50,34},{1,48}... | collective-permute-start | bytes 393224 | tf_op jit(solution)/shard_map/ppermute | solution.py:41
  106.1 3.2 %collective-permute-done.25.refs_1_ = bf16[2,64,512]{2,1,0:T(8,128)(2,1)S(1)} collective-permute-done((bf16[2,64,512]{2,1,0:T(8,128)(2,1)S(1)}, bf16[2,64,512]{2,1,0:T(8,128)(2,1)S(1)}, u32[]{:S(2)}, u32[]{:S(2)}) %collective-permute-start.25) | collective-permute-done | bytes 131104 | tf_op jit(solution)/shard_map/ppermute | solution.py:49
  110.8 6.0 %collective-permute-start.28 = (bf16[4,2,64,512]{3,2,1,0:T(8,128)(2,1)S(1)}, bf16[4,2,64,512]{3,2,1,0:T(8,128)(2,1)S(1)}, u32[]{:S(2)}, u32[]{:S(2)}) collective-permute-start(bf16[4,2,64,512]{3,2,1,0:T(8,128)(2,1)S(1)} %stack.39.refs_0_), channel_id=1, source_target_pairs={{0,128},{2,130},{16,144},{18,146},{32,160},{34,162},{48,176},{50,1... | collective-permute-start | bytes 1572872 | tf_op jit(solution)/shard_map/ppermute | solution.py:33
  116.9 2.8 %collective-permute-start.20 = (bf16[2,64,512]{2,1,0:T(8,128)(2,1)S(1)}, bf16[2,64,512]{2,1,0:T(8,128)(2,1)S(1)}, u32[]{:S(2)}, u32[]{:S(2)}) collective-permute-start(bf16[2,64,512]{2,1,0:T(8,128)(2,1)S(1)} %pad_maximum_fusion.refs_0_), channel_id=1, source_target_pairs={{0,64},{2,66},{16,80},{18,82},{32,96},{34,98},{48,112},{50,114},{1... | collective-permute-start | bytes 393224 | tf_op jit(solution)/shard_map/ppermute | solution.py:33
  119.7 2.0 %collective-permute-start.29 = (bf16[4,2,64,512]{3,2,1,0:T(8,128)(2,1)S(1)}, bf16[4,2,64,512]{3,2,1,0:T(8,128)(2,1)S(1)}, u32[]{:S(2)}, u32[]{:S(2)}) collective-permute-start(bf16[4,2,64,512]{3,2,1,0:T(8,128)(2,1)S(1)} %stack.39.refs_0_), channel_id=1, source_target_pairs={{0,64},{2,66},{16,80},{18,82},{32,96},{34,98},{48,112},{50,114},{1... | collective-permute-start | bytes 1572872 | tf_op jit(solution)/shard_map/ppermute | solution.py:33
  121.8 10.1 %collective-permute-done.19.refs_1_ = bf16[2,64,512]{2,1,0:T(8,128)(2,1)S(1)} collective-permute-done((bf16[2,64,512]{2,1,0:T(8,128)(2,1)S(1)}, bf16[2,64,512]{2,1,0:T(8,128)(2,1)S(1)}, u32[]{:S(2)}, u32[]{:S(2)}) %collective-permute-start.19) | collective-permute-done | bytes 131104 | tf_op jit(solution)/shard_map/ppermute | solution.py:33
  131.9 1.9 %collective-permute-start.30 = (bf16[4,2,64,512]{3,2,1,0:T(8,128)(2,1)S(1)}, bf16[4,2,64,512]{3,2,1,0:T(8,128)(2,1)S(1)}, u32[]{:S(2)}, u32[]{:S(2)}) collective-permute-start(bf16[4,2,64,512]{3,2,1,0:T(8,128)(2,1)S(1)} %stack.39.refs_0_), channel_id=1, source_target_pairs={{0,192},{2,194},{16,208},{18,210},{32,224},{34,226},{48,240},{50,2... | collective-permute-start | bytes 1572872 | tf_op jit(solution)/shard_map/ppermute | solution.py:33
  133.8 2.8 %collective-permute-done.20.refs_2_ = bf16[2,64,512]{2,1,0:T(8,128)(2,1)S(1)} collective-permute-done((bf16[2,64,512]{2,1,0:T(8,128)(2,1)S(1)}, bf16[2,64,512]{2,1,0:T(8,128)(2,1)S(1)}, u32[]{:S(2)}, u32[]{:S(2)}) %collective-permute-start.20) | collective-permute-done | bytes 131104 | tf_op jit(solution)/shard_map/ppermute | solution.py:33
  138.0 1.2 collective-permute-start.23
  139.2 2.1 %collective-permute-start.24 = (bf16[4,2,64,512]{3,2,1,0:T(8,128)(2,1)S(1)}, bf16[4,2,64,512]{3,2,1,0:T(8,128)(2,1)S(1)}, u32[]{:S(2)}, u32[]{:S(2)}) collective-permute-start(bf16[4,2,64,512]{3,2,1,0:T(8,128)(2,1)S(1)} %stack.38.refs_0_), channel_id=1, source_target_pairs={{0,49},{2,51},{16,0},{18,2},{32,16},{34,18},{48,32},{50,34},{1,48}... | collective-permute-start | bytes 1572872 | tf_op jit(solution)/shard_map/ppermute | solution.py:41
  141.2 1.2 collective-permute-done.29.refs_2_
  142.5 2.1 %project.3 = (f32[256,384]{1,0:T(8,128)S(1)}, bf16[512,2048]{1,0:T(8,128)(2,1)S(1)}) custom-call(s32[5]{0:T(128)S(1)} %stack.33.place, bf16[4,2,64,512]{3,2,1,0:T(8,128)(2,1)S(1)} %stack.39.refs_0_, bf16[4,2,64,512]{3,2,1,0:T(8,128)(2,1)S(1)} %collective-permute-done.28.refs_1_, bf16[4,2,64,512]{3,2,1,0:T(8,128)(2,1)S(1)} %collective-permute-done.29.refs_2_, ...), custom_call_target="tpu_custom_call" | custom-call | flops 536870912 | bytes 1048576 | tf_op jit(solution)/shard_map/project/pallas_call | solution.py:248
  144.7 8.8 %collective-permute-done.22.refs_1_ = bf16[4,2,64,512]{3,2,1,0:T(8,128)(2,1)S(1)} collective-permute-done((bf16[4,2,64,512]{3,2,1,0:T(8,128)(2,1)S(1)}, bf16[4,2,64,512]{3,2,1,0:T(8,128)(2,1)S(1)}, u32[]{:S(2)}, u32[]{:S(2)}) %collective-permute-start.22) | collective-permute-done | bytes 524320 | tf_op jit(solution)/shard_map/ppermute | solution.py:49
  153.5 6.2 %collective-permute-done.23.refs_2_ = bf16[4,2,64,512]{3,2,1,0:T(8,128)(2,1)S(1)} collective-permute-done((bf16[4,2,64,512]{3,2,1,0:T(8,128)(2,1)S(1)}, bf16[4,2,64,512]{3,2,1,0:T(8,128)(2,1)S(1)}, u32[]{:S(2)}, u32[]{:S(2)}) %collective-permute-start.23) | collective-permute-done | bytes 524320 | tf_op jit(solution)/shard_map/ppermute | solution.py:41
  159.7 2.1 %project.2 = (f32[256,384]{1,0:T(8,128)S(1)}, bf16[512,2048]{1,0:T(8,128)(2,1)S(1)}) custom-call(s32[5]{0:T(128)S(1)} %stack.33.place, bf16[4,2,64,512]{3,2,1,0:T(8,128)(2,1)S(1)} %stack.38.refs_0_, bf16[4,2,64,512]{3,2,1,0:T(8,128)(2,1)S(1)} %collective-permute-done.22.refs_1_, bf16[4,2,64,512]{3,2,1,0:T(8,128)(2,1)S(1)} %collective-permute-done.23.refs_2_, ...), custom_call_target="tpu_custom_call" | custom-call | flops 536870912 | bytes 1048576 | tf_op jit(solution)/shard_map/project/pallas_call | solution.py:248
  163.8 1.0 collective-permute-start.33
  164.8 3.2 %collective-permute-start.34 = (f32[2,64,384]{2,1,0:T(8,128)S(1)}, f32[2,64,384]{2,1,0:T(8,128)S(1)}, u32[]{:S(2)}, u32[]{:S(2)}) collective-permute-start(f32[2,64,384]{2,1,0:T(8,128)S(1)} %get-tuple-element.41), channel_id=1, source_target_pairs={{0,4},{2,6},{16,20},{18,22},{32,36},{34,38},{48,52},{50,54},{1,5},... | collective-permute-start | bytes 589832 | tf_op jit(solution)/shard_map/ppermute | solution.py:37
  167.9 1.1 collective-permute-start.35
  169.1 4.1 %collective-permute-done.33.p1 = f32[2,64,384]{2,1,0:T(8,128)S(1)} collective-permute-done((f32[2,64,384]{2,1,0:T(8,128)S(1)}, f32[2,64,384]{2,1,0:T(8,128)S(1)}, u32[]{:S(2)}, u32[]{:S(2)}) %collective-permute-start.33) | collective-permute-done | bytes 196640 | tf_op jit(solution)/shard_map/ppermute | solution.py:37
  173.2 3.5 %collective-permute-done.34.p2 = f32[2,64,384]{2,1,0:T(8,128)S(1)} collective-permute-done((f32[2,64,384]{2,1,0:T(8,128)S(1)}, f32[2,64,384]{2,1,0:T(8,128)S(1)}, u32[]{:S(2)}, u32[]{:S(2)}) %collective-permute-start.34) | collective-permute-done | bytes 196640 | tf_op jit(solution)/shard_map/ppermute | solution.py:37
  (62 shorter events, 15.5 us)
Async XLA Ops:
  0.0 48.3 %copy-start = (bf16[512,2048]{1,0:T(8,128)(2,1)S(1)}, bf16[512,2048]{1,0:T(8,128)(2,1)}, u32[]{:S(2)}) copy-start(bf16[512,2048]{1,0:T(8,128)(2,1)} %right.3) | copy-start | bytes 6291460
  0.0 9.9 %collective-permute-start.6 = (bf16[32,2048]{1,0:T(8,128)(2,1)}, bf16[32,2048]{1,0:T(8,128)(2,1)S(1)}, u32[]{:S(2)}, u32[]{:S(2)}) collective-permute-start(bf16[32,2048]{1,0:T(8,128)(2,1)} %refs_0_.2), channel_id=1, source_target_pairs={{0,32},{2,35},{16,48},{18,51},{32,1},{34,2},{48,17},{50,18},{1,33}... | collective-permute-start | bytes 393224 | tf_op jit(solution)/shard_map/ppermute | solution.py:49
  3.3 10.0 %collective-permute-start.7 = (bf16[32,2048]{1,0:T(8,128)(2,1)}, bf16[32,2048]{1,0:T(8,128)(2,1)S(1)}, u32[]{:S(2)}, u32[]{:S(2)}) collective-permute-start(bf16[32,2048]{1,0:T(8,128)(2,1)} %refs_0_.2), channel_id=1, source_target_pairs={{0,16},{2,18},{16,32},{18,34},{32,48},{34,50},{48,1},{50,3},{1,17}... | collective-permute-start | bytes 393224 | tf_op jit(solution)/shard_map/ppermute | solution.py:41
  5.2 8.0 %collective-permute-start.8 = (bf16[32,2048]{1,0:T(8,128)(2,1)}, bf16[32,2048]{1,0:T(8,128)(2,1)S(1)}, u32[]{:S(2)}, u32[]{:S(2)}) collective-permute-start(bf16[32,2048]{1,0:T(8,128)(2,1)} %refs_0_.2), channel_id=1, source_target_pairs={{0,49},{2,51},{16,0},{18,2},{32,16},{34,18},{48,32},{50,34},{1,48}... | collective-permute-start | bytes 393224 | tf_op jit(solution)/shard_map/ppermute | solution.py:41
  13.2 0.9 copy-start.4
  14.8 24.1 %collective-permute-start.10 = (bf16[4,32,2048]{2,1,0:T(8,128)(2,1)S(1)}, bf16[4,32,2048]{2,1,0:T(8,128)(2,1)S(1)}, u32[]{:S(2)}, u32[]{:S(2)}) collective-permute-start(bf16[4,32,2048]{2,1,0:T(8,128)(2,1)S(1)} %stack.37.refs_0_), channel_id=1, source_target_pairs={{0,64},{2,66},{16,80},{18,82},{32,96},{34,98},{48,112},{50,114},{1... | collective-permute-start | bytes 1572872 | tf_op jit(solution)/shard_map/ppermute | solution.py:33
  16.5 8.1 %collective-permute-start = (bf16[32,2048]{1,0:T(8,128)(2,1)}, bf16[32,2048]{1,0:T(8,128)(2,1)S(1)}, u32[]{:S(2)}, u32[]{:S(2)}) collective-permute-start(bf16[32,2048]{1,0:T(8,128)(2,1)} %refs_0_.1), channel_id=1, source_target_pairs={{0,128},{2,130},{16,144},{18,146},{32,160},{34,162},{48,176},{50,1... | collective-permute-start | bytes 393224 | tf_op jit(solution)/shard_map/ppermute | solution.py:33
  17.6 16.3 %collective-permute-start.1 = (bf16[32,2048]{1,0:T(8,128)(2,1)}, bf16[32,2048]{1,0:T(8,128)(2,1)S(1)}, u32[]{:S(2)}, u32[]{:S(2)}) collective-permute-start(bf16[32,2048]{1,0:T(8,128)(2,1)} %refs_0_.1), channel_id=1, source_target_pairs={{0,64},{2,66},{16,80},{18,82},{32,96},{34,98},{48,112},{50,114},{1... | collective-permute-start | bytes 393224 | tf_op jit(solution)/shard_map/ppermute | solution.py:33
  18.5 15.4 %collective-permute-start.2 = (bf16[32,2048]{1,0:T(8,128)(2,1)}, bf16[32,2048]{1,0:T(8,128)(2,1)S(1)}, u32[]{:S(2)}, u32[]{:S(2)}) collective-permute-start(bf16[32,2048]{1,0:T(8,128)(2,1)} %refs_0_.1), channel_id=1, source_target_pairs={{0,192},{2,194},{16,208},{18,210},{32,224},{34,226},{48,240},{50,2... | collective-permute-start | bytes 393224 | tf_op jit(solution)/shard_map/ppermute | solution.py:33
  19.8 20.2 %collective-permute-start.11 = (bf16[4,32,2048]{2,1,0:T(8,128)(2,1)S(1)}, bf16[4,32,2048]{2,1,0:T(8,128)(2,1)S(1)}, u32[]{:S(2)}, u32[]{:S(2)}) collective-permute-start(bf16[4,32,2048]{2,1,0:T(8,128)(2,1)S(1)} %stack.37.refs_0_), channel_id=1, source_target_pairs={{0,192},{2,194},{16,208},{18,210},{32,224},{34,226},{48,240},{50,2... | collective-permute-start | bytes 1572872 | tf_op jit(solution)/shard_map/ppermute | solution.py:33
  24.6 23.8 %collective-permute-start.9 = (bf16[4,32,2048]{2,1,0:T(8,128)(2,1)S(1)}, bf16[4,32,2048]{2,1,0:T(8,128)(2,1)S(1)}, u32[]{:S(2)}, u32[]{:S(2)}) collective-permute-start(bf16[4,32,2048]{2,1,0:T(8,128)(2,1)S(1)} %stack.37.refs_0_), channel_id=1, source_target_pairs={{0,128},{2,130},{16,144},{18,146},{32,160},{34,162},{48,176},{50,1... | collective-permute-start | bytes 1572872 | tf_op jit(solution)/shard_map/ppermute | solution.py:33
  33.9 0.9 copy-start.5
  35.5 27.3 %copy-start.1 = (bf16[512,2048]{1,0:T(8,128)(2,1)S(1)}, bf16[512,2048]{1,0:T(8,128)(2,1)}, u32[]{:S(2)}) copy-start(bf16[512,2048]{1,0:T(8,128)(2,1)} %right.2) | copy-start | bytes 6291460
  35.5 21.8 %collective-permute-start.3 = (bf16[4,32,2048]{2,1,0:T(8,128)(2,1)S(1)}, bf16[4,32,2048]{2,1,0:T(8,128)(2,1)S(1)}, u32[]{:S(2)}, u32[]{:S(2)}) collective-permute-start(bf16[4,32,2048]{2,1,0:T(8,128)(2,1)S(1)} %stack.36.refs_0_), channel_id=1, source_target_pairs={{0,32},{2,35},{16,48},{18,51},{32,1},{34,2},{48,17},{50,18},{1,33}... | collective-permute-start | bytes 1572872 | tf_op jit(solution)/shard_map/ppermute | solution.py:49
  36.7 26.1 %collective-permute-start.4 = (bf16[4,32,2048]{2,1,0:T(8,128)(2,1)S(1)}, bf16[4,32,2048]{2,1,0:T(8,128)(2,1)S(1)}, u32[]{:S(2)}, u32[]{:S(2)}) collective-permute-start(bf16[4,32,2048]{2,1,0:T(8,128)(2,1)S(1)} %stack.36.refs_0_), channel_id=1, source_target_pairs={{0,16},{2,18},{16,32},{18,34},{32,48},{34,50},{48,1},{50,3},{1,17}... | collective-permute-start | bytes 1572872 | tf_op jit(solution)/shard_map/ppermute | solution.py:41
  38.9 23.9 %collective-permute-start.5 = (bf16[4,32,2048]{2,1,0:T(8,128)(2,1)S(1)}, bf16[4,32,2048]{2,1,0:T(8,128)(2,1)S(1)}, u32[]{:S(2)}, u32[]{:S(2)}) collective-permute-start(bf16[4,32,2048]{2,1,0:T(8,128)(2,1)S(1)} %stack.36.refs_0_), channel_id=1, source_target_pairs={{0,49},{2,51},{16,0},{18,2},{32,16},{34,18},{48,32},{50,34},{1,48}... | collective-permute-start | bytes 1572872 | tf_op jit(solution)/shard_map/ppermute | solution.py:41
  48.3 0.7 copy-start.6
  53.8 16.0 %collective-permute-start.13 = (f32[256,512]{1,0:T(8,128)S(1)}, f32[256,512]{1,0:T(8,128)S(1)}, u32[]{:S(2)}, u32[]{:S(2)}) collective-permute-start(f32[256,512]{1,0:T(8,128)S(1)} %get-tuple-element.30), channel_id=1, source_target_pairs={{0,2},{2,0},{16,18},{18,16},{32,34},{34,32},{48,50},{50,48},{1,3},... | collective-permute-start | bytes 1572872 | tf_op jit(solution)/shard_map/ppermute | solution.py:45
  67.5 2.2 %collective-permute-start.12 = (f32[256,512]{1,0:T(8,128)S(1)}, f32[256,512]{1,0:T(8,128)S(1)}, u32[]{:S(2)}, u32[]{:S(2)}) collective-permute-start(f32[256,512]{1,0:T(8,128)S(1)} %get-tuple-element.29), channel_id=1, source_target_pairs={{0,2},{2,0},{16,18},{18,16},{32,34},{34,32},{48,50},{50,48},{1,3},... | collective-permute-start | bytes 1572872 | tf_op jit(solution)/shard_map/ppermute | solution.py:45
  69.9 10.8 %collective-permute-start.14 = (f32[2,64,512]{2,1,0:T(8,128)S(1)}, f32[2,64,512]{2,1,0:T(8,128)S(1)}, u32[]{:S(2)}, u32[]{:S(2)}) collective-permute-start(f32[2,64,512]{2,1,0:T(8,128)S(1)} %get-tuple-element.32), channel_id=1, source_target_pairs={{0,8},{2,10},{16,24},{18,26},{32,40},{34,42},{48,56},{50,58},{1,9}... | collective-permute-start | bytes 786440 | tf_op jit(solution)/shard_map/ppermute | solution.py:37
  73.2 12.6 %collective-permute-start.15 = (f32[2,64,512]{2,1,0:T(8,128)S(1)}, f32[2,64,512]{2,1,0:T(8,128)S(1)}, u32[]{:S(2)}, u32[]{:S(2)}) collective-permute-start(f32[2,64,512]{2,1,0:T(8,128)S(1)} %get-tuple-element.33), channel_id=1, source_target_pairs={{0,4},{2,6},{16,20},{18,22},{32,36},{34,38},{48,52},{50,54},{1,5},... | collective-permute-start | bytes 786440 | tf_op jit(solution)/shard_map/ppermute | solution.py:37
  73.8 12.3 %collective-permute-start.16 = (f32[2,64,512]{2,1,0:T(8,128)S(1)}, f32[2,64,512]{2,1,0:T(8,128)S(1)}, u32[]{:S(2)}, u32[]{:S(2)}) collective-permute-start(f32[2,64,512]{2,1,0:T(8,128)S(1)} %get-tuple-element.34), channel_id=1, source_target_pairs={{0,12},{2,14},{16,28},{18,30},{32,44},{34,46},{48,60},{50,62},{1,1... | collective-permute-start | bytes 786440 | tf_op jit(solution)/shard_map/ppermute | solution.py:37
  86.2 56.3 %copy-start.2 = (bf16[384,2048]{1,0:T(8,128)(2,1)S(1)}, bf16[384,2048]{1,0:T(8,128)(2,1)}, u32[]{:S(2)}) copy-start(bf16[384,2048]{1,0:T(8,128)(2,1)} %tok.3) | copy-start | bytes 4718596
  86.3 7.9 %collective-permute-start.17 = (bf16[2,64,512]{2,1,0:T(8,128)(2,1)S(1)}, bf16[2,64,512]{2,1,0:T(8,128)(2,1)S(1)}, u32[]{:S(2)}, u32[]{:S(2)}) collective-permute-start(bf16[2,64,512]{2,1,0:T(8,128)(2,1)S(1)} %factor_sum.1), channel_id=1, source_target_pairs={{0,0},{2,32},{16,16},{18,48},{32,2},{34,34},{48,18},{50,50},{1,1},... | collective-permute-start | bytes 393224 | tf_op jit(solution)/shard_map/ppermute | solution.py:57
  89.7 10.8 %collective-permute-start.18 = (bf16[2,64,512]{2,1,0:T(8,128)(2,1)S(1)}, bf16[2,64,512]{2,1,0:T(8,128)(2,1)S(1)}, u32[]{:S(2)}, u32[]{:S(2)}) collective-permute-start(bf16[2,64,512]{2,1,0:T(8,128)(2,1)S(1)} %factor_sum.1), channel_id=1, source_target_pairs={{0,1},{2,33},{16,17},{18,49},{32,3},{34,35},{48,19},{50,51},{1,0},... | collective-permute-start | bytes 393224 | tf_op jit(solution)/shard_map/ppermute | solution.py:57
  100.5 8.8 %collective-permute-start.25 = (bf16[2,64,512]{2,1,0:T(8,128)(2,1)S(1)}, bf16[2,64,512]{2,1,0:T(8,128)(2,1)S(1)}, u32[]{:S(2)}, u32[]{:S(2)}) collective-permute-start(bf16[2,64,512]{2,1,0:T(8,128)(2,1)S(1)} %pad_maximum_fusion.1.refs_0_), channel_id=1, source_target_pairs={{0,32},{2,35},{16,48},{18,51},{32,1},{34,2},{48,17},{50,18},{1,33}... | collective-permute-start | bytes 393224 | tf_op jit(solution)/shard_map/ppermute | solution.py:49
  102.8 7.2 %collective-permute-start.26 = (bf16[2,64,512]{2,1,0:T(8,128)(2,1)S(1)}, bf16[2,64,512]{2,1,0:T(8,128)(2,1)S(1)}, u32[]{:S(2)}, u32[]{:S(2)}) collective-permute-start(bf16[2,64,512]{2,1,0:T(8,128)(2,1)S(1)} %pad_maximum_fusion.1.refs_0_), channel_id=1, source_target_pairs={{0,16},{2,18},{16,32},{18,34},{32,48},{34,50},{48,1},{50,3},{1,17}... | collective-permute-start | bytes 393224 | tf_op jit(solution)/shard_map/ppermute | solution.py:41
  102.8 7.2 %collective-permute-start.27 = (bf16[2,64,512]{2,1,0:T(8,128)(2,1)S(1)}, bf16[2,64,512]{2,1,0:T(8,128)(2,1)S(1)}, u32[]{:S(2)}, u32[]{:S(2)}) collective-permute-start(bf16[2,64,512]{2,1,0:T(8,128)(2,1)S(1)} %pad_maximum_fusion.1.refs_0_), channel_id=1, source_target_pairs={{0,49},{2,51},{16,0},{18,2},{32,16},{34,18},{48,32},{50,34},{1,48}... | collective-permute-start | bytes 393224 | tf_op jit(solution)/shard_map/ppermute | solution.py:41
  110.8 28.4 %collective-permute-start.28 = (bf16[4,2,64,512]{3,2,1,0:T(8,128)(2,1)S(1)}, bf16[4,2,64,512]{3,2,1,0:T(8,128)(2,1)S(1)}, u32[]{:S(2)}, u32[]{:S(2)}) collective-permute-start(bf16[4,2,64,512]{3,2,1,0:T(8,128)(2,1)S(1)} %stack.39.refs_0_), channel_id=1, source_target_pairs={{0,128},{2,130},{16,144},{18,146},{32,160},{34,162},{48,176},{50,1... | collective-permute-start | bytes 1572872 | tf_op jit(solution)/shard_map/ppermute | solution.py:33
  116.8 15.1 %collective-permute-start.19 = (bf16[2,64,512]{2,1,0:T(8,128)(2,1)S(1)}, bf16[2,64,512]{2,1,0:T(8,128)(2,1)S(1)}, u32[]{:S(2)}, u32[]{:S(2)}) collective-permute-start(bf16[2,64,512]{2,1,0:T(8,128)(2,1)S(1)} %pad_maximum_fusion.refs_0_), channel_id=1, source_target_pairs={{0,128},{2,130},{16,144},{18,146},{32,160},{34,162},{48,176},{50,1... | collective-permute-start | bytes 393224 | tf_op jit(solution)/shard_map/ppermute | solution.py:33
  116.9 19.7 %collective-permute-start.20 = (bf16[2,64,512]{2,1,0:T(8,128)(2,1)S(1)}, bf16[2,64,512]{2,1,0:T(8,128)(2,1)S(1)}, u32[]{:S(2)}, u32[]{:S(2)}) collective-permute-start(bf16[2,64,512]{2,1,0:T(8,128)(2,1)S(1)} %pad_maximum_fusion.refs_0_), channel_id=1, source_target_pairs={{0,64},{2,66},{16,80},{18,82},{32,96},{34,98},{48,112},{50,114},{1... | collective-permute-start | bytes 393224 | tf_op jit(solution)/shard_map/ppermute | solution.py:33
  119.7 16.8 %collective-permute-start.21 = (bf16[2,64,512]{2,1,0:T(8,128)(2,1)S(1)}, bf16[2,64,512]{2,1,0:T(8,128)(2,1)S(1)}, u32[]{:S(2)}, u32[]{:S(2)}) collective-permute-start(bf16[2,64,512]{2,1,0:T(8,128)(2,1)S(1)} %pad_maximum_fusion.refs_0_), channel_id=1, source_target_pairs={{0,192},{2,194},{16,208},{18,210},{32,224},{34,226},{48,240},{50,2... | collective-permute-start | bytes 393224 | tf_op jit(solution)/shard_map/ppermute | solution.py:33
  119.7 22.7 %collective-permute-start.29 = (bf16[4,2,64,512]{3,2,1,0:T(8,128)(2,1)S(1)}, bf16[4,2,64,512]{3,2,1,0:T(8,128)(2,1)S(1)}, u32[]{:S(2)}, u32[]{:S(2)}) collective-permute-start(bf16[4,2,64,512]{3,2,1,0:T(8,128)(2,1)S(1)} %stack.39.refs_0_), channel_id=1, source_target_pairs={{0,64},{2,66},{16,80},{18,82},{32,96},{34,98},{48,112},{50,114},{1... | collective-permute-start | bytes 1572872 | tf_op jit(solution)/shard_map/ppermute | solution.py:33
  131.9 10.5 %collective-permute-start.30 = (bf16[4,2,64,512]{3,2,1,0:T(8,128)(2,1)S(1)}, bf16[4,2,64,512]{3,2,1,0:T(8,128)(2,1)S(1)}, u32[]{:S(2)}, u32[]{:S(2)}) collective-permute-start(bf16[4,2,64,512]{3,2,1,0:T(8,128)(2,1)S(1)} %stack.39.refs_0_), channel_id=1, source_target_pairs={{0,192},{2,194},{16,208},{18,210},{32,224},{34,226},{48,240},{50,2... | collective-permute-start | bytes 1572872 | tf_op jit(solution)/shard_map/ppermute | solution.py:33
  137.3 22.5 %copy-start.3 = (bf16[384,2048]{1,0:T(8,128)(2,1)S(1)}, bf16[384,2048]{1,0:T(8,128)(2,1)}, u32[]{:S(2)}) copy-start(bf16[384,2048]{1,0:T(8,128)(2,1)} %tok.2) | copy-start | bytes 4718596
  137.3 16.2 %collective-permute-start.22 = (bf16[4,2,64,512]{3,2,1,0:T(8,128)(2,1)S(1)}, bf16[4,2,64,512]{3,2,1,0:T(8,128)(2,1)S(1)}, u32[]{:S(2)}, u32[]{:S(2)}) collective-permute-start(bf16[4,2,64,512]{3,2,1,0:T(8,128)(2,1)S(1)} %stack.38.refs_0_), channel_id=1, source_target_pairs={{0,32},{2,35},{16,48},{18,51},{32,1},{34,2},{48,17},{50,18},{1,33}... | collective-permute-start | bytes 1572872 | tf_op jit(solution)/shard_map/ppermute | solution.py:49
  138.0 21.7 %collective-permute-start.23 = (bf16[4,2,64,512]{3,2,1,0:T(8,128)(2,1)S(1)}, bf16[4,2,64,512]{3,2,1,0:T(8,128)(2,1)S(1)}, u32[]{:S(2)}, u32[]{:S(2)}) collective-permute-start(bf16[4,2,64,512]{3,2,1,0:T(8,128)(2,1)S(1)} %stack.38.refs_0_), channel_id=1, source_target_pairs={{0,16},{2,18},{16,32},{18,34},{32,48},{34,50},{48,1},{50,3},{1,17}... | collective-permute-start | bytes 1572872 | tf_op jit(solution)/shard_map/ppermute | solution.py:41
  139.2 20.6 %collective-permute-start.24 = (bf16[4,2,64,512]{3,2,1,0:T(8,128)(2,1)S(1)}, bf16[4,2,64,512]{3,2,1,0:T(8,128)(2,1)S(1)}, u32[]{:S(2)}, u32[]{:S(2)}) collective-permute-start(bf16[4,2,64,512]{3,2,1,0:T(8,128)(2,1)S(1)} %stack.38.refs_0_), channel_id=1, source_target_pairs={{0,49},{2,51},{16,0},{18,2},{32,16},{34,18},{48,32},{50,34},{1,48}... | collective-permute-start | bytes 1572872 | tf_op jit(solution)/shard_map/ppermute | solution.py:41
  144.6 18.9 %collective-permute-start.32 = (f32[256,384]{1,0:T(8,128)S(1)}, f32[256,384]{1,0:T(8,128)S(1)}, u32[]{:S(2)}, u32[]{:S(2)}) collective-permute-start(f32[256,384]{1,0:T(8,128)S(1)} %get-tuple-element.38), channel_id=1, source_target_pairs={{0,2},{2,0},{16,18},{18,16},{32,34},{34,32},{48,50},{50,48},{1,3},... | collective-permute-start | bytes 1179656 | tf_op jit(solution)/shard_map/ppermute | solution.py:45
  161.9 1.8 %collective-permute-start.31 = (f32[256,384]{1,0:T(8,128)S(1)}, f32[256,384]{1,0:T(8,128)S(1)}, u32[]{:S(2)}, u32[]{:S(2)}) collective-permute-start(f32[256,384]{1,0:T(8,128)S(1)} %get-tuple-element.37), channel_id=1, source_target_pairs={{0,2},{2,0},{16,18},{18,16},{32,34},{34,32},{48,50},{50,48},{1,3},... | collective-permute-start | bytes 1179656 | tf_op jit(solution)/shard_map/ppermute | solution.py:45
  162.7 6.4 %copy-start.7 = (s32[384]{0:T(512)S(1)}, s32[384]{0:T(512)}, u32[]{:S(2)}) copy-start(s32[384]{0:T(512)} %param.15) | copy-start | bytes 4612
  163.8 9.4 %collective-permute-start.33 = (f32[2,64,384]{2,1,0:T(8,128)S(1)}, f32[2,64,384]{2,1,0:T(8,128)S(1)}, u32[]{:S(2)}, u32[]{:S(2)}) collective-permute-start(f32[2,64,384]{2,1,0:T(8,128)S(1)} %get-tuple-element.40), channel_id=1, source_target_pairs={{0,8},{2,10},{16,24},{18,26},{32,40},{34,42},{48,56},{50,58},{1,9}... | collective-permute-start | bytes 589832 | tf_op jit(solution)/shard_map/ppermute | solution.py:37
  164.8 11.9 %collective-permute-start.34 = (f32[2,64,384]{2,1,0:T(8,128)S(1)}, f32[2,64,384]{2,1,0:T(8,128)S(1)}, u32[]{:S(2)}, u32[]{:S(2)}) collective-permute-start(f32[2,64,384]{2,1,0:T(8,128)S(1)} %get-tuple-element.41), channel_id=1, source_target_pairs={{0,4},{2,6},{16,20},{18,22},{32,36},{34,38},{48,52},{50,54},{1,5},... | collective-permute-start | bytes 589832 | tf_op jit(solution)/shard_map/ppermute | solution.py:37
  167.9 9.3 %collective-permute-start.35 = (f32[2,64,384]{2,1,0:T(8,128)S(1)}, f32[2,64,384]{2,1,0:T(8,128)S(1)}, u32[]{:S(2)}, u32[]{:S(2)}) collective-permute-start(f32[2,64,384]{2,1,0:T(8,128)S(1)} %get-tuple-element.42), channel_id=1, source_target_pairs={{0,12},{2,14},{16,28},{18,30},{32,44},{34,46},{48,60},{50,62},{1,1... | collective-permute-start | bytes 589832 | tf_op jit(solution)/shard_map/ppermute | solution.py:37
where the time goes:
time: 179 us; the launch traced here: 178 us
  waiting for transfers between devices  94.9 us (53%)
  starting transfers between devices  59.3 us (33%)
  Pallas kernels  20.8 us (12%)
  local copies, waits for them, and re-layouts  2.6 us (1%)
    ppermute x12, waiting for transfers between devices, along_x(): lax.ppermute(value, AXES, move(lambda x, y, z, c: (x + step, y, z, c)))  32.6 us
    ppermute x12, starting transfers between devices, along_x(): lax.ppermute(value, AXES, move(lambda x, y, z, c: (x + step, y, z, c)))  21.8 us
    ppermute x4, waiting for transfers between devices, far_z(): lax.ppermute(value, AXES, move(lambda x, y, z, c: (x, y, z + 2 - 4 * c, c)))  18.9 us
    ppermute x6, waiting for transfers between devices, along_y(): lax.ppermute(value, AXES, move(lambda x, y, z, c: (x, y + step, z, c)))  17.9 us
    ppermute x8, waiting for transfers between devices, along_z(): lax.ppermute(value, AXES, move(lambda x, y, z, c: (x, y, z + step, c)))  15.8 us
    ppermute x8, starting transfers between devices, along_z(): lax.ppermute(value, AXES, move(lambda x, y, z, c: (x, y, z + step, c)))  12.9 us
    ppermute x6, starting transfers between devices, along_y(): lax.ppermute(value, AXES, move(lambda x, y, z, c: (x, y + step, z, c)))  11.8 us
    pallas_call x2, Pallas kernels, precondition(): pl.pallas_call(functools.partial(precondition_kernel, z_first), out_shape...  9.49 us
  transfers between devices with their start and end apart: 36, of which 23 were waited for; matrix products, arithmetic and copies ran while one was open for 0% of the time, Pallas kernels for 10%

commit v1 on v0

--- a/solution.py
+++ b/solution.py
@@ -63,10 +63,6 @@
 
 def smem():
     return pl.BlockSpec(memory_space=pltpu.SMEM)
-
-
-def anywhere():
-    return pl.BlockSpec(memory_space=pl.ANY)
 
 
 def chunk_row(slot_pair, y, c):
@@ -105,19 +101,13 @@
 
 
 def precondition_kernel(z_first, place, slots, *refs):
-    bundles, (inv, send, rows, sem) = refs[:4], refs[4:]
+    bundles, (inv, send, rows) = refs[:4], refs[4:]
     x, y, z, c = place[0], place[1], place[2], place[3]
-    copies = []
     for second, first, dx, dz in piece_offsets(z_first, c):
         query = lax.rem(x + dx + 4, 4) * 4 + lax.rem(z + dz + 8, 4)
         slot = slots[query]
         row = chunk_row(lax.div(slot, 2), y, c) + 32 * lax.rem(slot, 2)
-        target = rows.at[pl.ds(pl.multiple_of(row, 32), 32), :]
-        copy = pltpu.make_async_copy(bundles[second].at[first], target, sem)
-        copy.start()
-        copies.append(copy)
-    for copy in copies:
-        copy.wait()
+        rows[pl.ds(pl.multiple_of(row, 32), 32), :] = bundles[second][first]
     tiles(send, rows, inv, 0)
 
 
@@ -136,9 +126,8 @@
             jax.ShapeDtypeStruct((256, 512), F32),
             jax.ShapeDtypeStruct((512, 2048), BF16),
         ),
-        in_specs=[smem(), smem()] + [anywhere()] * 4 + [vmem()],
+        in_specs=[smem(), smem()] + [vmem()] * 5,
         out_specs=(vmem(),) * 2,
-        scratch_shapes=[pltpu.SemaphoreType.DMA(())],
         compiler_params=limit(8),
         cost_estimate=estimate(),
         name="precondition",
@@ -156,46 +145,44 @@
     )(rows, right)
 
 
-def stack_kernel(*refs):
-    sources, (out, sems) = refs[:-2], refs[-2:]
-    copies = [
-        pltpu.make_async_copy(source, out.at[i], sems.at[i]) for i, source in enumerate(sources)
-    ]
-    for copy in copies:
-        copy.start()
-    for copy in copies:
-        copy.wait()
-
-
-def stack(*arrays):
-    count = len(arrays)
-    return pl.pallas_call(
-        stack_kernel,
-        out_shape=jax.ShapeDtypeStruct((count,) + arrays[0].shape, arrays[0].dtype),
-        in_specs=[anywhere()] * count,
-        out_specs=vmem(),
-        scratch_shapes=[pltpu.SemaphoreType.DMA((count,))],
-        compiler_params=limit(2),
-        name="stack",
-    )(*arrays)
-
-
 def limit(mib):
     return pltpu.CompilerParams(vmem_limit_bytes=mib << 20)
 
 
-def split_kernel(keep_a, keep_g, got_a, got_g, *outs):
-    for step, out in enumerate(outs):
+BITS = 14
+
+
+def code(values):
+    largest = jnp.max(jnp.abs(values), axis=(0, 1), keepdims=True)
+    power = jnp.ceil(jnp.log2(jnp.maximum(largest, 1e-30)))
+    whole = jnp.floor(values * jnp.exp2(BITS - power) + 0.5)
+    return whole.astype(jnp.int32), jnp.broadcast_to(power, (8, values.shape[1])).astype(jnp.int32)
+
+
+def coded(block, array):
+    power = block[128 + 8 * array : 136 + 8 * array, :].astype(jnp.int32).astype(F32)[:1]
+    whole = block[64 * array : 64 * array + 64, :].astype(jnp.int32).astype(F32)
+    return whole * jnp.exp2(power - BITS)
+
+
+def split_kernel(keep_a, keep_g, got_a, got_g, own, *outs):
+    for step in range(4):
         rows = slice(64 * step, 64 * step + 64)
-        out[0] = keep_a[rows, :] + got_a[rows, :]
-        out[1] = keep_g[rows, :] + got_g[rows, :]
+        sums = keep_a[rows, :] + got_a[rows, :], keep_g[rows, :] + got_g[rows, :]
+        if step == 0:
+            own[0], own[1] = sums
+        else:
+            (acts, power_a), (grads, power_g) = map(code, sums)
+            block = jnp.concatenate([acts, grads, power_a, power_g], axis=0)
+            outs[step - 1][...] = block.astype(jnp.int16)
 
 
 def split(keep, got):
-    shape = jax.ShapeDtypeStruct((2, 64, keep[0].shape[-1]), F32)
+    width = keep[0].shape[-1]
     return pl.pallas_call(
         split_kernel,
-        out_shape=(shape,) * 4,
+        out_shape=(jax.ShapeDtypeStruct((2, 64, width), F32),)
+        + (jax.ShapeDtypeStruct((144, width), jnp.int16),) * 3,
         in_specs=[vmem()] * 4,
         out_specs=(vmem(),) * 4,
         compiler_params=limit(6),
@@ -203,8 +190,13 @@
     )(*keep, *got)
 
 
+def total(p0, p1, p2, p3, array):
+    return (p0[array] + coded(p1, array)) + (coded(p2, array) + coded(p3, array))
+
+
 def factor_kernel(p0, p1, p2, p3, out):
-    out[...] = ((p0[...] + p1[...]) + (p2[...] + p3[...])).astype(BF16)
+    for array in range(2):
+        out[array] = total(p0, p1, p2, p3, array).astype(BF16)
 
 
 def factor_sum(parts):
@@ -219,24 +211,17 @@
 
 
 def project_kernel(z_first, place, *refs):
-    bundles, (tok, send, factor, sem) = refs[:4], refs[4:]
+    bundles, (tok, send, factor) = refs[:4], refs[4:]
     x, y, c = place[0], place[1], place[3]
     ring = place[4]
-    copies = []
     for second, first, dx, dz in piece_offsets(z_first, c):
         for high in range(2):
             px = lax.rem(x + dx - y + 8, 4)
             pz = lax.rem(ring + dz + 4 * high + 8, 8)
             row = chunk_row(2 * px + lax.rem(lax.div(pz, 2), 2), y, c)
             column = (2 * lax.rem(pz, 2) + lax.div(pz, 4)) * 512
-            target = factor.at[
-                pl.ds(pl.multiple_of(row, 64), 64), pl.ds(pl.multiple_of(column, 512), 512)
-            ]
-            copy = pltpu.make_async_copy(bundles[second].at[first, high], target, sem)
-            copy.start()
-            copies.append(copy)
-    for copy in copies:
-        copy.wait()
+            at = pl.ds(pl.multiple_of(row, 64), 64), pl.ds(pl.multiple_of(column, 512), 512)
+            factor[at] = bundles[second][first, high]
     send[...] = nt_dot(factor[:256, :], tok[...])
 
 
@@ -251,9 +236,8 @@
             jax.ShapeDtypeStruct((256, tok.shape[0]), F32),
             jax.ShapeDtypeStruct((512, 2048), BF16),
         ),
-        in_specs=[smem()] + [anywhere()] * 4 + [vmem()],
+        in_specs=[smem()] + [vmem()] * 5,
         out_specs=(vmem(),) * 2,
-        scratch_shapes=[pltpu.SemaphoreType.DMA(())],
         compiler_params=limit(8),
         cost_estimate=estimate(),
         name="project",
@@ -261,14 +245,12 @@
 
 
 def score_kernel(p0, p1, p2, p3, resident, out):
-    acts = (p0[0] + p1[0]) + (p2[0] + p3[0])
-    grads = (p0[1] + p1[1]) + (p2[1] + p3[1])
-    product = acts * grads
+    product = total(p0, p1, p2, p3, 0) * total(p0, p1, p2, p3, 1)
     scale = 1.0 / (D * math.sqrt(QTOK))
     here = resident[...].astype(F32)
     for query in range(2):
-        total = jnp.sum(product[QTOK * query : QTOK * query + QTOK], axis=0, keepdims=True)
-        out[query : query + 1, :] = total * scale * here
+        summed = jnp.sum(product[QTOK * query : QTOK * query + QTOK], axis=0, keepdims=True)
+        out[query : query + 1, :] = summed * scale * here
 
 
 def score(parts, resident):
@@ -311,7 +293,7 @@
 
     def gather(acts, grads):
         ax, gz = x_others(acts), z_others(grads)
-        ax, gz = stack(acts, *ax), stack(grads, *gz)
+        ax, gz = jnp.stack([acts] + ax), jnp.stack([grads] + gz)
         gzx = [gz] + x_others(gz)
         axz = [ax] + z_others(ax)
         return axz, gzx

time: 179 us -> 165 us (0.922)
  Pallas kernels: 20.8 us -> 11.7 us
  waiting for transfers between devices: 94.9 us -> 91 us
  local copies, waits for them, and re-layouts: 2.6 us -> 0.13 us
  other arithmetic: 0.03 us -> 2.12 us
    ppermute x6, waiting for transfers between devices: 17.9 us -> 10.4 us  [along_y(): lax.ppermute(value, AXES, move(lambda x, y, z, c: (x, y + step, z, c)))]
    pallas_call x2, Pallas kernels: 9.49 us -> 3.75 us  [precondition(): pl.pallas_call(functools.partial(precondition_kernel, z_first), out_shape...]
    unnamed x16 -> x12, local copies, waits for them, and re-layouts: 2.49 us -> 0.03 us
    pallas_call x6 -> x2, Pallas kernels: 3 us -> 0.69 us  [split(): pl.pallas_call(split_kernel, out_shape=(jax.ShapeDtypeStruct((2, 64, widt...]
    another operation x2 -> x6, other arithmetic: 0.03 us -> 2.12 us  [gather(): ax, gz = (jnp.stack([acts] + ax), jnp.stack([grads] + gz))]
  transfers between devices with their start and end apart: 36 -> 36, of which waited for: 23 -> 24; matrix products, arithmetic and copies ran while one was open for 0% -> 1% of each run, Pallas kernels for 10% -> 6%
where the time goes in v1:
time: 165 us; the launch traced here: 164 us
  waiting for transfers between devices  91 us (55%)
  starting transfers between devices  58.8 us (36%)
  Pallas kernels  11.7 us (7%)
  other arithmetic  2.12 us (1%)
    ppermute x12, waiting for transfers between devices, along_x(): lax.ppermute(value, AXES, move(lambda x, y, z, c: (x + step, y, z, c)))  33.7 us
    ppermute x12, starting transfers between devices, along_x(): lax.ppermute(value, AXES, move(lambda x, y, z, c: (x + step, y, z, c)))  22.1 us
    ppermute x4, waiting for transfers between devices, far_z(): lax.ppermute(value, AXES, move(lambda x, y, z, c: (x, y, z + 2 - 4 * c, c)))  20.5 us
    ppermute x8, waiting for transfers between devices, along_z(): lax.ppermute(value, AXES, move(lambda x, y, z, c: (x, y, z + step, c)))  16.6 us
    ppermute x8, starting transfers between devices, along_z(): lax.ppermute(value, AXES, move(lambda x, y, z, c: (x, y, z + step, c)))  12.9 us
    ppermute x6, starting transfers between devices, along_y(): lax.ppermute(value, AXES, move(lambda x, y, z, c: (x, y + step, z, c)))  10.9 us
    ppermute x6, waiting for transfers between devices, along_y(): lax.ppermute(value, AXES, move(lambda x, y, z, c: (x, y + step, z, c)))  10.4 us
    ppermute x2, waiting for transfers between devices, to_owner(): return lax.ppermute(value, AXES, move(target))  9.48 us
  transfers between devices with their start and end apart: 36, of which 24 were waited for; matrix products, arithmetic and copies ran while one was open for 1% of the time, Pallas kernels for 6%

profile of v1, /device:TPU:2, one launch (start us, length us, event | category | flops | bytes accessed | tf_op | source)
XLA Modules:
  0.0 163.9 jit_solution(9547795266197719706)
XLA Ops:
  0.0 3.3 %collective-permute-start.6 = (bf16[32,2048]{1,0:T(8,128)(2,1)}, bf16[32,2048]{1,0:T(8,128)(2,1)S(1)}, u32[]{:S(2)}, u32[]{:S(2)}) collective-permute-start(bf16[32,2048]{1,0:T(8,128)(2,1)} %param.11), channel_id=1, source_target_pairs={{0,32},{2,35},{16,48},{18,51},{32,1},{34,2},{48,17},{50,18},{1,33}... | collective-permute-start | bytes 393224 | tf_op jit(solution)/shard_map/ppermute | solution.py:49
  3.3 1.9 %collective-permute-start.7 = (bf16[32,2048]{1,0:T(8,128)(2,1)}, bf16[32,2048]{1,0:T(8,128)(2,1)S(1)}, u32[]{:S(2)}, u32[]{:S(2)}) collective-permute-start(bf16[32,2048]{1,0:T(8,128)(2,1)} %param.11), channel_id=1, source_target_pairs={{0,16},{2,18},{16,32},{18,34},{32,48},{34,50},{48,1},{50,3},{1,17}... | collective-permute-start | bytes 393224 | tf_op jit(solution)/shard_map/ppermute | solution.py:41
  5.2 1.3 collective-permute-start.8
  6.5 3.4 %collective-permute-done.6 = bf16[32,2048]{1,0:T(8,128)(2,1)S(1)} collective-permute-done((bf16[32,2048]{1,0:T(8,128)(2,1)}, bf16[32,2048]{1,0:T(8,128)(2,1)S(1)}, u32[]{:S(2)}, u32[]{:S(2)}) %collective-permute-start.6) | collective-permute-done | bytes 131104 | tf_op jit(solution)/shard_map/ppermute | solution.py:49
  9.9 3.3 %collective-permute-done.7 = bf16[32,2048]{1,0:T(8,128)(2,1)S(1)} collective-permute-done((bf16[32,2048]{1,0:T(8,128)(2,1)}, bf16[32,2048]{1,0:T(8,128)(2,1)S(1)}, u32[]{:S(2)}, u32[]{:S(2)}) %collective-permute-start.7) | collective-permute-done | bytes 131104 | tf_op jit(solution)/shard_map/ppermute | solution.py:41
  13.2 1.0 pad_maximum_fusion.1.refs_0_
  14.2 1.6 collective-permute-start.10
  15.9 1.1 collective-permute-start
  17.9 1.3 collective-permute-start.2
  19.1 3.2 %collective-permute-start.11 = (bf16[4,32,2048]{2,1,0:T(8,128)(2,1)S(1)}, bf16[4,32,2048]{2,1,0:T(8,128)(2,1)S(1)}, u32[]{:S(2)}, u32[]{:S(2)}) collective-permute-start(bf16[4,32,2048]{2,1,0:T(8,128)(2,1)S(1)} %pad_maximum_fusion.1.refs_0_), channel_id=1, source_target_pairs={{0,192},{2,194},{16,208},{18,210},{32,224},{34,226},{48,240},{50,2... | collective-permute-start | bytes 1572872 | tf_op jit(solution)/shard_map/ppermute | solution.py:33
  22.4 1.6 collective-permute-done
  24.9 8.4 %collective-permute-done.1 = bf16[32,2048]{1,0:T(8,128)(2,1)S(1)} collective-permute-done((bf16[32,2048]{1,0:T(8,128)(2,1)}, bf16[32,2048]{1,0:T(8,128)(2,1)S(1)}, u32[]{:S(2)}, u32[]{:S(2)}) %collective-permute-start.1) | collective-permute-done | bytes 131104 | tf_op jit(solution)/shard_map/ppermute | solution.py:33
  33.3 1.0 pad_maximum_fusion.refs_0_
  34.3 1.2 collective-permute-start.3
  35.5 2.2 %collective-permute-start.4 = (bf16[4,32,2048]{2,1,0:T(8,128)(2,1)S(1)}, bf16[4,32,2048]{2,1,0:T(8,128)(2,1)S(1)}, u32[]{:S(2)}, u32[]{:S(2)}) collective-permute-start(bf16[4,32,2048]{2,1,0:T(8,128)(2,1)S(1)} %pad_maximum_fusion.refs_0_), channel_id=1, source_target_pairs={{0,16},{2,18},{16,32},{18,34},{32,48},{34,50},{48,1},{50,3},{1,17}... | collective-permute-start | bytes 1572872 | tf_op jit(solution)/shard_map/ppermute | solution.py:41
  37.7 1.0 collective-permute-start.5
  38.7 9.0 %collective-permute-done.9.refs_1_ = bf16[4,32,2048]{2,1,0:T(8,128)(2,1)S(1)} collective-permute-done((bf16[4,32,2048]{2,1,0:T(8,128)(2,1)S(1)}, bf16[4,32,2048]{2,1,0:T(8,128)(2,1)S(1)}, u32[]{:S(2)}, u32[]{:S(2)}) %collective-permute-start.9) | collective-permute-done | bytes 524320 | tf_op jit(solution)/shard_map/ppermute | solution.py:33
  47.7 1.9 %precondition.3 = (f32[256,512]{1,0:T(8,128)S(1)}, bf16[512,2048]{1,0:T(8,128)(2,1)S(1)}) custom-call(s32[5]{0:T(128)S(1)} %stack.89.place, s32[16]{0:T(128)S(1)} %copy-done.4, bf16[4,32,2048]{2,1,0:T(8,128)(2,1)S(1)} %pad_maximum_fusion.1.refs_0_, bf16[4,32,2048]{2,1,0:T(8,128)(2,1)S(1)} %collective-permute-done.9.refs_1_, ...), custom_call_target="tpu_custom_call" | custom-call | flops 536870912 | bytes 1048576 | tf_op jit(solution)/shard_map/precondition/pallas_call | solution.py:123
  49.7 6.4 %collective-permute-done.3.refs_1_ = bf16[4,32,2048]{2,1,0:T(8,128)(2,1)S(1)} collective-permute-done((bf16[4,32,2048]{2,1,0:T(8,128)(2,1)S(1)}, bf16[4,32,2048]{2,1,0:T(8,128)(2,1)S(1)}, u32[]{:S(2)}, u32[]{:S(2)}) %collective-permute-start.3) | collective-permute-done | bytes 524320 | tf_op jit(solution)/shard_map/ppermute | solution.py:49
  56.1 5.5 %collective-permute-done.4.refs_2_ = bf16[4,32,2048]{2,1,0:T(8,128)(2,1)S(1)} collective-permute-done((bf16[4,32,2048]{2,1,0:T(8,128)(2,1)S(1)}, bf16[4,32,2048]{2,1,0:T(8,128)(2,1)S(1)}, u32[]{:S(2)}, u32[]{:S(2)}) %collective-permute-start.4) | collective-permute-done | bytes 524320 | tf_op jit(solution)/shard_map/ppermute | solution.py:41
  61.6 1.9 %precondition.2 = (f32[256,512]{1,0:T(8,128)S(1)}, bf16[512,2048]{1,0:T(8,128)(2,1)S(1)}) custom-call(s32[5]{0:T(128)S(1)} %stack.89.place, s32[16]{0:T(128)S(1)} %copy-done.4, bf16[4,32,2048]{2,1,0:T(8,128)(2,1)S(1)} %pad_maximum_fusion.refs_0_, bf16[4,32,2048]{2,1,0:T(8,128)(2,1)S(1)} %collective-permute-done.3.refs_1_, ...), custom_call_target="tpu_custom_call" | custom-call | flops 536870912 | bytes 1048576 | tf_op jit(solution)/shard_map/precondition/pallas_call | solution.py:123
  66.0 3.3 %collective-permute-start.14 = (s16[144,512]{1,0:T(8,128)(2,1)S(1)}, s16[144,512]{1,0:T(8,128)(2,1)S(1)}, u32[]{:S(2)}, u32[]{:S(2)}) collective-permute-start(s16[144,512]{1,0:T(8,128)(2,1)S(1)} %get-tuple-element.32), channel_id=1, source_target_pairs={{0,8},{2,10},{16,24},{18,26},{32,40},{34,42},{48,56},{50,58},{1,9}... | collective-permute-start | bytes 442376 | tf_op jit(solution)/shard_map/ppermute | solution.py:37
  70.0 2.6 %collective-permute-start.16 = (s16[144,512]{1,0:T(8,128)(2,1)S(1)}, s16[144,512]{1,0:T(8,128)(2,1)S(1)}, u32[]{:S(2)}, u32[]{:S(2)}) collective-permute-start(s16[144,512]{1,0:T(8,128)(2,1)S(1)} %get-tuple-element.34), channel_id=1, source_target_pairs={{0,12},{2,14},{16,28},{18,30},{32,44},{34,46},{48,60},{50,62},{1,1... | collective-permute-start | bytes 442376 | tf_op jit(solution)/shard_map/ppermute | solution.py:37
  72.6 1.8 %collective-permute-done.14.p1 = s16[144,512]{1,0:T(8,128)(2,1)S(1)} collective-permute-done((s16[144,512]{1,0:T(8,128)(2,1)S(1)}, s16[144,512]{1,0:T(8,128)(2,1)S(1)}, u32[]{:S(2)}, u32[]{:S(2)}) %collective-permute-start.14) | collective-permute-done | bytes 147488 | tf_op jit(solution)/shard_map/ppermute | solution.py:37
  74.3 2.7 %collective-permute-done.15.p2 = s16[144,512]{1,0:T(8,128)(2,1)S(1)} collective-permute-done((s16[144,512]{1,0:T(8,128)(2,1)S(1)}, s16[144,512]{1,0:T(8,128)(2,1)S(1)}, u32[]{:S(2)}, u32[]{:S(2)}) %collective-permute-start.15) | collective-permute-done | bytes 147488 | tf_op jit(solution)/shard_map/ppermute | solution.py:37
  77.5 3.4 %collective-permute-start.17 = (bf16[2,64,512]{2,1,0:T(8,128)(2,1)S(1)}, bf16[2,64,512]{2,1,0:T(8,128)(2,1)S(1)}, u32[]{:S(2)}, u32[]{:S(2)}) collective-permute-start(bf16[2,64,512]{2,1,0:T(8,128)(2,1)S(1)} %factor_sum.1), channel_id=1, source_target_pairs={{0,0},{2,32},{16,16},{18,48},{32,2},{34,34},{48,18},{50,50},{1,1},... | collective-permute-start | bytes 393224 | tf_op jit(solution)/shard_map/ppermute | solution.py:57
  81.0 1.3 collective-permute-start.18
  82.3 3.1 %collective-permute-done.17 = bf16[2,64,512]{2,1,0:T(8,128)(2,1)S(1)} collective-permute-done((bf16[2,64,512]{2,1,0:T(8,128)(2,1)S(1)}, bf16[2,64,512]{2,1,0:T(8,128)(2,1)S(1)}, u32[]{:S(2)}, u32[]{:S(2)}) %collective-permute-start.17) | collective-permute-done | bytes 131104 | tf_op jit(solution)/shard_map/ppermute | solution.py:57
  85.4 6.3 %collective-permute-done.18 = bf16[2,64,512]{2,1,0:T(8,128)(2,1)S(1)} collective-permute-done((bf16[2,64,512]{2,1,0:T(8,128)(2,1)S(1)}, bf16[2,64,512]{2,1,0:T(8,128)(2,1)S(1)}, u32[]{:S(2)}, u32[]{:S(2)}) %collective-permute-start.18) | collective-permute-done | bytes 131104 | tf_op jit(solution)/shard_map/ppermute | solution.py:57
  91.8 2.3 %collective-permute-start.25 = (bf16[2,64,512]{2,1,0:T(8,128)(2,1)S(1)}, bf16[2,64,512]{2,1,0:T(8,128)(2,1)S(1)}, u32[]{:S(2)}, u32[]{:S(2)}) collective-permute-start(bf16[2,64,512]{2,1,0:T(8,128)(2,1)S(1)} %get-tuple-element.44), channel_id=1, source_target_pairs={{0,32},{2,35},{16,48},{18,51},{32,1},{34,2},{48,17},{50,18},{1,33}... | collective-permute-start | bytes 393224 | tf_op jit(solution)/shard_map/ppermute | solution.py:49
  94.1 3.2 %collective-permute-start.27 = (bf16[2,64,512]{2,1,0:T(8,128)(2,1)S(1)}, bf16[2,64,512]{2,1,0:T(8,128)(2,1)S(1)}, u32[]{:S(2)}, u32[]{:S(2)}) collective-permute-start(bf16[2,64,512]{2,1,0:T(8,128)(2,1)S(1)} %get-tuple-element.44), channel_id=1, source_target_pairs={{0,49},{2,51},{16,0},{18,2},{32,16},{34,18},{48,32},{50,34},{1,48}... | collective-permute-start | bytes 393224 | tf_op jit(solution)/shard_map/ppermute | solution.py:41
  97.4 3.2 %collective-permute-done.25 = bf16[2,64,512]{2,1,0:T(8,128)(2,1)S(1)} collective-permute-done((bf16[2,64,512]{2,1,0:T(8,128)(2,1)S(1)}, bf16[2,64,512]{2,1,0:T(8,128)(2,1)S(1)}, u32[]{:S(2)}, u32[]{:S(2)}) %collective-permute-start.25) | collective-permute-done | bytes 131104 | tf_op jit(solution)/shard_map/ppermute | solution.py:49
  101.4 5.7 %collective-permute-start.28 = (bf16[4,2,64,512]{3,2,1,0:T(8,128)(2,1)S(1)}, bf16[4,2,64,512]{3,2,1,0:T(8,128)(2,1)S(1)}, u32[]{:S(2)}, u32[]{:S(2)}) collective-permute-start(bf16[4,2,64,512]{3,2,1,0:T(8,128)(2,1)S(1)} %pad_maximum_fusion.3.refs_0_), channel_id=1, source_target_pairs={{0,128},{2,130},{16,144},{18,146},{32,160},{34,162},{48,176},{50,1... | collective-permute-start | bytes 1572872 | tf_op jit(solution)/shard_map/ppermute | solution.py:33
  107.3 3.1 %collective-permute-start.20 = (bf16[2,64,512]{2,1,0:T(8,128)(2,1)S(1)}, bf16[2,64,512]{2,1,0:T(8,128)(2,1)S(1)}, u32[]{:S(2)}, u32[]{:S(2)}) collective-permute-start(bf16[2,64,512]{2,1,0:T(8,128)(2,1)S(1)} %get-tuple-element.50), channel_id=1, source_target_pairs={{0,64},{2,66},{16,80},{18,82},{32,96},{34,98},{48,112},{50,114},{1... | collective-permute-start | bytes 393224 | tf_op jit(solution)/shard_map/ppermute | solution.py:33
  110.4 2.0 %collective-permute-start.29 = (bf16[4,2,64,512]{3,2,1,0:T(8,128)(2,1)S(1)}, bf16[4,2,64,512]{3,2,1,0:T(8,128)(2,1)S(1)}, u32[]{:S(2)}, u32[]{:S(2)}) collective-permute-start(bf16[4,2,64,512]{3,2,1,0:T(8,128)(2,1)S(1)} %pad_maximum_fusion.3.refs_0_), channel_id=1, source_target_pairs={{0,64},{2,66},{16,80},{18,82},{32,96},{34,98},{48,112},{50,114},{1... | collective-permute-start | bytes 1572872 | tf_op jit(solution)/shard_map/ppermute | solution.py:33
  112.4 9.9 %collective-permute-done.19 = bf16[2,64,512]{2,1,0:T(8,128)(2,1)S(1)} collective-permute-done((bf16[2,64,512]{2,1,0:T(8,128)(2,1)S(1)}, bf16[2,64,512]{2,1,0:T(8,128)(2,1)S(1)}, u32[]{:S(2)}, u32[]{:S(2)}) %collective-permute-start.19) | collective-permute-done | bytes 131104 | tf_op jit(solution)/shard_map/ppermute | solution.py:33
  122.3 2.1 %collective-permute-start.30 = (bf16[4,2,64,512]{3,2,1,0:T(8,128)(2,1)S(1)}, bf16[4,2,64,512]{3,2,1,0:T(8,128)(2,1)S(1)}, u32[]{:S(2)}, u32[]{:S(2)}) collective-permute-start(bf16[4,2,64,512]{3,2,1,0:T(8,128)(2,1)S(1)} %pad_maximum_fusion.3.refs_0_), channel_id=1, source_target_pairs={{0,192},{2,194},{16,208},{18,210},{32,224},{34,226},{48,240},{50,2... | collective-permute-start | bytes 1572872 | tf_op jit(solution)/shard_map/ppermute | solution.py:33
  124.5 2.8 %collective-permute-done.20 = bf16[2,64,512]{2,1,0:T(8,128)(2,1)S(1)} collective-permute-done((bf16[2,64,512]{2,1,0:T(8,128)(2,1)S(1)}, bf16[2,64,512]{2,1,0:T(8,128)(2,1)S(1)}, u32[]{:S(2)}, u32[]{:S(2)}) %collective-permute-start.20) | collective-permute-done | bytes 131104 | tf_op jit(solution)/shard_map/ppermute | solution.py:33
  128.0 1.2 collective-permute-start.23
  129.2 2.1 %collective-permute-start.24 = (bf16[4,2,64,512]{3,2,1,0:T(8,128)(2,1)S(1)}, bf16[4,2,64,512]{3,2,1,0:T(8,128)(2,1)S(1)}, u32[]{:S(2)}, u32[]{:S(2)}) collective-permute-start(bf16[4,2,64,512]{3,2,1,0:T(8,128)(2,1)S(1)} %pad_maximum_fusion.2.refs_0_), channel_id=1, source_target_pairs={{0,49},{2,51},{16,0},{18,2},{32,16},{34,18},{48,32},{50,34},{1,48}... | collective-permute-start | bytes 1572872 | tf_op jit(solution)/shard_map/ppermute | solution.py:41
  131.3 1.8 %collective-permute-done.29.refs_2_ = bf16[4,2,64,512]{3,2,1,0:T(8,128)(2,1)S(1)} collective-permute-done((bf16[4,2,64,512]{3,2,1,0:T(8,128)(2,1)S(1)}, bf16[4,2,64,512]{3,2,1,0:T(8,128)(2,1)S(1)}, u32[]{:S(2)}, u32[]{:S(2)}) %collective-permute-start.29) | collective-permute-done | bytes 524320 | tf_op jit(solution)/shard_map/ppermute | solution.py:33
  133.2 1.5 project.3
  134.9 7.5 %collective-permute-done.22.refs_1_ = bf16[4,2,64,512]{3,2,1,0:T(8,128)(2,1)S(1)} collective-permute-done((bf16[4,2,64,512]{3,2,1,0:T(8,128)(2,1)S(1)}, bf16[4,2,64,512]{3,2,1,0:T(8,128)(2,1)S(1)}, u32[]{:S(2)}, u32[]{:S(2)}) %collective-permute-start.22) | collective-permute-done | bytes 524320 | tf_op jit(solution)/shard_map/ppermute | solution.py:49
  142.4 7.1 %collective-permute-done.23.refs_2_ = bf16[4,2,64,512]{3,2,1,0:T(8,128)(2,1)S(1)} collective-permute-done((bf16[4,2,64,512]{3,2,1,0:T(8,128)(2,1)S(1)}, bf16[4,2,64,512]{3,2,1,0:T(8,128)(2,1)S(1)}, u32[]{:S(2)}, u32[]{:S(2)}) %collective-permute-start.23) | collective-permute-done | bytes 524320 | tf_op jit(solution)/shard_map/ppermute | solution.py:41
  149.5 1.5 project.2
  154.1 3.5 %collective-permute-start.34 = (s16[144,384]{1,0:T(8,128)(2,1)S(1)}, s16[144,384]{1,0:T(8,128)(2,1)S(1)}, u32[]{:S(2)}, u32[]{:S(2)}) collective-permute-start(s16[144,384]{1,0:T(8,128)(2,1)S(1)} %get-tuple-element.41), channel_id=1, source_target_pairs={{0,4},{2,6},{16,20},{18,22},{32,36},{34,38},{48,52},{50,54},{1,5},... | collective-permute-start | bytes 331784 | tf_op jit(solution)/shard_map/ppermute | solution.py:37
  157.6 3.0 %collective-permute-done.33.p1 = s16[144,384]{1,0:T(8,128)(2,1)S(1)} collective-permute-done((s16[144,384]{1,0:T(8,128)(2,1)S(1)}, s16[144,384]{1,0:T(8,128)(2,1)S(1)}, u32[]{:S(2)}, u32[]{:S(2)}) %collective-permute-start.33) | collective-permute-done | bytes 110624 | tf_op jit(solution)/shard_map/ppermute | solution.py:37
  160.6 1.8 %collective-permute-done.34.p2 = s16[144,384]{1,0:T(8,128)(2,1)S(1)} collective-permute-done((s16[144,384]{1,0:T(8,128)(2,1)S(1)}, s16[144,384]{1,0:T(8,128)(2,1)S(1)}, u32[]{:S(2)}, u32[]{:S(2)}) %collective-permute-start.34) | collective-permute-done | bytes 110624 | tf_op jit(solution)/shard_map/ppermute | solution.py:37
  (58 shorter events, 12.2 us)
Async XLA Ops:
  0.0 47.7 %copy-start.4 = (s32[16]{0:T(128)S(1)}, s32[16]{0:T(128)}, u32[]{:S(2)}) copy-start(s32[16]{0:T(128)} %slots.1) | copy-start | bytes 196
  0.0 47.7 %copy-start = (bf16[512,2048]{1,0:T(8,128)(2,1)S(1)}, bf16[512,2048]{1,0:T(8,128)(2,1)}, u32[]{:S(2)}) copy-start(bf16[512,2048]{1,0:T(8,128)(2,1)} %right.3) | copy-start | bytes 6291460
  0.0 9.9 %collective-permute-start.6 = (bf16[32,2048]{1,0:T(8,128)(2,1)}, bf16[32,2048]{1,0:T(8,128)(2,1)S(1)}, u32[]{:S(2)}, u32[]{:S(2)}) collective-permute-start(bf16[32,2048]{1,0:T(8,128)(2,1)} %param.11), channel_id=1, source_target_pairs={{0,32},{2,35},{16,48},{18,51},{32,1},{34,2},{48,17},{50,18},{1,33}... | collective-permute-start | bytes 393224 | tf_op jit(solution)/shard_map/ppermute | solution.py:49
  3.3 10.0 %collective-permute-start.7 = (bf16[32,2048]{1,0:T(8,128)(2,1)}, bf16[32,2048]{1,0:T(8,128)(2,1)S(1)}, u32[]{:S(2)}, u32[]{:S(2)}) collective-permute-start(bf16[32,2048]{1,0:T(8,128)(2,1)} %param.11), channel_id=1, source_target_pairs={{0,16},{2,18},{16,32},{18,34},{32,48},{34,50},{48,1},{50,3},{1,17}... | collective-permute-start | bytes 393224 | tf_op jit(solution)/shard_map/ppermute | solution.py:41
  5.2 8.0 %collective-permute-start.8 = (bf16[32,2048]{1,0:T(8,128)(2,1)}, bf16[32,2048]{1,0:T(8,128)(2,1)S(1)}, u32[]{:S(2)}, u32[]{:S(2)}) collective-permute-start(bf16[32,2048]{1,0:T(8,128)(2,1)} %param.11), channel_id=1, source_target_pairs={{0,49},{2,51},{16,0},{18,2},{32,16},{34,18},{48,32},{50,34},{1,48}... | collective-permute-start | bytes 393224 | tf_op jit(solution)/shard_map/ppermute | solution.py:41
  14.2 23.4 %collective-permute-start.10 = (bf16[4,32,2048]{2,1,0:T(8,128)(2,1)S(1)}, bf16[4,32,2048]{2,1,0:T(8,128)(2,1)S(1)}, u32[]{:S(2)}, u32[]{:S(2)}) collective-permute-start(bf16[4,32,2048]{2,1,0:T(8,128)(2,1)S(1)} %pad_maximum_fusion.1.refs_0_), channel_id=1, source_target_pairs={{0,64},{2,66},{16,80},{18,82},{32,96},{34,98},{48,112},{50,114},{1... | collective-permute-start | bytes 1572872 | tf_op jit(solution)/shard_map/ppermute | solution.py:33
  15.9 8.1 %collective-permute-start = (bf16[32,2048]{1,0:T(8,128)(2,1)}, bf16[32,2048]{1,0:T(8,128)(2,1)S(1)}, u32[]{:S(2)}, u32[]{:S(2)}) collective-permute-start(bf16[32,2048]{1,0:T(8,128)(2,1)} %param.10), channel_id=1, source_target_pairs={{0,128},{2,130},{16,144},{18,146},{32,160},{34,162},{48,176},{50,1... | collective-permute-start | bytes 393224 | tf_op jit(solution)/shard_map/ppermute | solution.py:33
  17.0 16.3 %collective-permute-start.1 = (bf16[32,2048]{1,0:T(8,128)(2,1)}, bf16[32,2048]{1,0:T(8,128)(2,1)S(1)}, u32[]{:S(2)}, u32[]{:S(2)}) collective-permute-start(bf16[32,2048]{1,0:T(8,128)(2,1)} %param.10), channel_id=1, source_target_pairs={{0,64},{2,66},{16,80},{18,82},{32,96},{34,98},{48,112},{50,114},{1... | collective-permute-start | bytes 393224 | tf_op jit(solution)/shard_map/ppermute | solution.py:33
  17.9 15.4 %collective-permute-start.2 = (bf16[32,2048]{1,0:T(8,128)(2,1)}, bf16[32,2048]{1,0:T(8,128)(2,1)S(1)}, u32[]{:S(2)}, u32[]{:S(2)}) collective-permute-start(bf16[32,2048]{1,0:T(8,128)(2,1)} %param.10), channel_id=1, source_target_pairs={{0,192},{2,194},{16,208},{18,210},{32,224},{34,226},{48,240},{50,2... | collective-permute-start | bytes 393224 | tf_op jit(solution)/shard_map/ppermute | solution.py:33
  19.1 19.6 %collective-permute-start.11 = (bf16[4,32,2048]{2,1,0:T(8,128)(2,1)S(1)}, bf16[4,32,2048]{2,1,0:T(8,128)(2,1)S(1)}, u32[]{:S(2)}, u32[]{:S(2)}) collective-permute-start(bf16[4,32,2048]{2,1,0:T(8,128)(2,1)S(1)} %pad_maximum_fusion.1.refs_0_), channel_id=1, source_target_pairs={{0,192},{2,194},{16,208},{18,210},{32,224},{34,226},{48,240},{50,2... | collective-permute-start | bytes 1572872 | tf_op jit(solution)/shard_map/ppermute | solution.py:33
  24.0 23.8 %collective-permute-start.9 = (bf16[4,32,2048]{2,1,0:T(8,128)(2,1)S(1)}, bf16[4,32,2048]{2,1,0:T(8,128)(2,1)S(1)}, u32[]{:S(2)}, u32[]{:S(2)}) collective-permute-start(bf16[4,32,2048]{2,1,0:T(8,128)(2,1)S(1)} %pad_maximum_fusion.1.refs_0_), channel_id=1, source_target_pairs={{0,128},{2,130},{16,144},{18,146},{32,160},{34,162},{48,176},{50,1... | collective-permute-start | bytes 1572872 | tf_op jit(solution)/shard_map/ppermute | solution.py:33
  34.3 27.3 %copy-start.1 = (bf16[512,2048]{1,0:T(8,128)(2,1)S(1)}, bf16[512,2048]{1,0:T(8,128)(2,1)}, u32[]{:S(2)}) copy-start(bf16[512,2048]{1,0:T(8,128)(2,1)} %right.2) | copy-start | bytes 6291460
  34.3 21.8 %collective-permute-start.3 = (bf16[4,32,2048]{2,1,0:T(8,128)(2,1)S(1)}, bf16[4,32,2048]{2,1,0:T(8,128)(2,1)S(1)}, u32[]{:S(2)}, u32[]{:S(2)}) collective-permute-start(bf16[4,32,2048]{2,1,0:T(8,128)(2,1)S(1)} %pad_maximum_fusion.refs_0_), channel_id=1, source_target_pairs={{0,32},{2,35},{16,48},{18,51},{32,1},{34,2},{48,17},{50,18},{1,33}... | collective-permute-start | bytes 1572872 | tf_op jit(solution)/shard_map/ppermute | solution.py:49
  35.5 26.1 %collective-permute-start.4 = (bf16[4,32,2048]{2,1,0:T(8,128)(2,1)S(1)}, bf16[4,32,2048]{2,1,0:T(8,128)(2,1)S(1)}, u32[]{:S(2)}, u32[]{:S(2)}) collective-permute-start(bf16[4,32,2048]{2,1,0:T(8,128)(2,1)S(1)} %pad_maximum_fusion.refs_0_), channel_id=1, source_target_pairs={{0,16},{2,18},{16,32},{18,34},{32,48},{34,50},{48,1},{50,3},{1,17}... | collective-permute-start | bytes 1572872 | tf_op jit(solution)/shard_map/ppermute | solution.py:41
  37.7 23.9 %collective-permute-start.5 = (bf16[4,32,2048]{2,1,0:T(8,128)(2,1)S(1)}, bf16[4,32,2048]{2,1,0:T(8,128)(2,1)S(1)}, u32[]{:S(2)}, u32[]{:S(2)}) collective-permute-start(bf16[4,32,2048]{2,1,0:T(8,128)(2,1)S(1)} %pad_maximum_fusion.refs_0_), channel_id=1, source_target_pairs={{0,49},{2,51},{16,0},{18,2},{32,16},{34,18},{48,32},{50,34},{1,48}... | collective-permute-start | bytes 1572872 | tf_op jit(solution)/shard_map/ppermute | solution.py:41
  49.6 16.0 %collective-permute-start.13 = (f32[256,512]{1,0:T(8,128)S(1)}, f32[256,512]{1,0:T(8,128)S(1)}, u32[]{:S(2)}, u32[]{:S(2)}) collective-permute-start(f32[256,512]{1,0:T(8,128)S(1)} %get-tuple-element.30), channel_id=1, source_target_pairs={{0,2},{2,0},{16,18},{18,16},{32,34},{34,32},{48,50},{50,48},{1,3},... | collective-permute-start | bytes 1572872 | tf_op jit(solution)/shard_map/ppermute | solution.py:45
  63.4 2.2 %collective-permute-start.12 = (f32[256,512]{1,0:T(8,128)S(1)}, f32[256,512]{1,0:T(8,128)S(1)}, u32[]{:S(2)}, u32[]{:S(2)}) collective-permute-start(f32[256,512]{1,0:T(8,128)S(1)} %get-tuple-element.29), channel_id=1, source_target_pairs={{0,2},{2,0},{16,18},{18,16},{32,34},{34,32},{48,50},{50,48},{1,3},... | collective-permute-start | bytes 1572872 | tf_op jit(solution)/shard_map/ppermute | solution.py:45
  66.0 8.3 %collective-permute-start.14 = (s16[144,512]{1,0:T(8,128)(2,1)S(1)}, s16[144,512]{1,0:T(8,128)(2,1)S(1)}, u32[]{:S(2)}, u32[]{:S(2)}) collective-permute-start(s16[144,512]{1,0:T(8,128)(2,1)S(1)} %get-tuple-element.32), channel_id=1, source_target_pairs={{0,8},{2,10},{16,24},{18,26},{32,40},{34,42},{48,56},{50,58},{1,9}... | collective-permute-start | bytes 442376 | tf_op jit(solution)/shard_map/ppermute | solution.py:37
  69.3 7.7 %collective-permute-start.15 = (s16[144,512]{1,0:T(8,128)(2,1)S(1)}, s16[144,512]{1,0:T(8,128)(2,1)S(1)}, u32[]{:S(2)}, u32[]{:S(2)}) collective-permute-start(s16[144,512]{1,0:T(8,128)(2,1)S(1)} %get-tuple-element.33), channel_id=1, source_target_pairs={{0,4},{2,6},{16,20},{18,22},{32,36},{34,38},{48,52},{50,54},{1,5},... | collective-permute-start | bytes 442376 | tf_op jit(solution)/shard_map/ppermute | solution.py:37
  70.0 7.4 %collective-permute-start.16 = (s16[144,512]{1,0:T(8,128)(2,1)S(1)}, s16[144,512]{1,0:T(8,128)(2,1)S(1)}, u32[]{:S(2)}, u32[]{:S(2)}) collective-permute-start(s16[144,512]{1,0:T(8,128)(2,1)S(1)} %get-tuple-element.34), channel_id=1, source_target_pairs={{0,12},{2,14},{16,28},{18,30},{32,44},{34,46},{48,60},{50,62},{1,1... | collective-permute-start | bytes 442376 | tf_op jit(solution)/shard_map/ppermute | solution.py:37
  77.4 55.9 %copy-start.2 = (bf16[384,2048]{1,0:T(8,128)(2,1)S(1)}, bf16[384,2048]{1,0:T(8,128)(2,1)}, u32[]{:S(2)}) copy-start(bf16[384,2048]{1,0:T(8,128)(2,1)} %tok.3) | copy-start | bytes 4718596
  77.5 7.9 %collective-permute-start.17 = (bf16[2,64,512]{2,1,0:T(8,128)(2,1)S(1)}, bf16[2,64,512]{2,1,0:T(8,128)(2,1)S(1)}, u32[]{:S(2)}, u32[]{:S(2)}) collective-permute-start(bf16[2,64,512]{2,1,0:T(8,128)(2,1)S(1)} %factor_sum.1), channel_id=1, source_target_pairs={{0,0},{2,32},{16,16},{18,48},{32,2},{34,34},{48,18},{50,50},{1,1},... | collective-permute-start | bytes 393224 | tf_op jit(solution)/shard_map/ppermute | solution.py:57
  81.0 10.8 %collective-permute-start.18 = (bf16[2,64,512]{2,1,0:T(8,128)(2,1)S(1)}, bf16[2,64,512]{2,1,0:T(8,128)(2,1)S(1)}, u32[]{:S(2)}, u32[]{:S(2)}) collective-permute-start(bf16[2,64,512]{2,1,0:T(8,128)(2,1)S(1)} %factor_sum.1), channel_id=1, source_target_pairs={{0,1},{2,33},{16,17},{18,49},{32,3},{34,35},{48,19},{50,51},{1,0},... | collective-permute-start | bytes 393224 | tf_op jit(solution)/shard_map/ppermute | solution.py:57
  91.8 8.8 %collective-permute-start.25 = (bf16[2,64,512]{2,1,0:T(8,128)(2,1)S(1)}, bf16[2,64,512]{2,1,0:T(8,128)(2,1)S(1)}, u32[]{:S(2)}, u32[]{:S(2)}) collective-permute-start(bf16[2,64,512]{2,1,0:T(8,128)(2,1)S(1)} %get-tuple-element.44), channel_id=1, source_target_pairs={{0,32},{2,35},{16,48},{18,51},{32,1},{34,2},{48,17},{50,18},{1,33}... | collective-permute-start | bytes 393224 | tf_op jit(solution)/shard_map/ppermute | solution.py:49
  94.1 7.2 %collective-permute-start.26 = (bf16[2,64,512]{2,1,0:T(8,128)(2,1)S(1)}, bf16[2,64,512]{2,1,0:T(8,128)(2,1)S(1)}, u32[]{:S(2)}, u32[]{:S(2)}) collective-permute-start(bf16[2,64,512]{2,1,0:T(8,128)(2,1)S(1)} %get-tuple-element.44), channel_id=1, source_target_pairs={{0,16},{2,18},{16,32},{18,34},{32,48},{34,50},{48,1},{50,3},{1,17}... | collective-permute-start | bytes 393224 | tf_op jit(solution)/shard_map/ppermute | solution.py:41
  94.1 7.2 %collective-permute-start.27 = (bf16[2,64,512]{2,1,0:T(8,128)(2,1)S(1)}, bf16[2,64,512]{2,1,0:T(8,128)(2,1)S(1)}, u32[]{:S(2)}, u32[]{:S(2)}) collective-permute-start(bf16[2,64,512]{2,1,0:T(8,128)(2,1)S(1)} %get-tuple-element.44), channel_id=1, source_target_pairs={{0,49},{2,51},{16,0},{18,2},{32,16},{34,18},{48,32},{50,34},{1,48}... | collective-permute-start | bytes 393224 | tf_op jit(solution)/shard_map/ppermute | solution.py:41
  101.4 27.8 %collective-permute-start.28 = (bf16[4,2,64,512]{3,2,1,0:T(8,128)(2,1)S(1)}, bf16[4,2,64,512]{3,2,1,0:T(8,128)(2,1)S(1)}, u32[]{:S(2)}, u32[]{:S(2)}) collective-permute-start(bf16[4,2,64,512]{3,2,1,0:T(8,128)(2,1)S(1)} %pad_maximum_fusion.3.refs_0_), channel_id=1, source_target_pairs={{0,128},{2,130},{16,144},{18,146},{32,160},{34,162},{48,176},{50,1... | collective-permute-start | bytes 1572872 | tf_op jit(solution)/shard_map/ppermute | solution.py:33
  107.2 15.1 %collective-permute-start.19 = (bf16[2,64,512]{2,1,0:T(8,128)(2,1)S(1)}, bf16[2,64,512]{2,1,0:T(8,128)(2,1)S(1)}, u32[]{:S(2)}, u32[]{:S(2)}) collective-permute-start(bf16[2,64,512]{2,1,0:T(8,128)(2,1)S(1)} %get-tuple-element.50), channel_id=1, source_target_pairs={{0,128},{2,130},{16,144},{18,146},{32,160},{34,162},{48,176},{50,1... | collective-permute-start | bytes 393224 | tf_op jit(solution)/shard_map/ppermute | solution.py:33
  107.3 19.9 %collective-permute-start.20 = (bf16[2,64,512]{2,1,0:T(8,128)(2,1)S(1)}, bf16[2,64,512]{2,1,0:T(8,128)(2,1)S(1)}, u32[]{:S(2)}, u32[]{:S(2)}) collective-permute-start(bf16[2,64,512]{2,1,0:T(8,128)(2,1)S(1)} %get-tuple-element.50), channel_id=1, source_target_pairs={{0,64},{2,66},{16,80},{18,82},{32,96},{34,98},{48,112},{50,114},{1... | collective-permute-start | bytes 393224 | tf_op jit(solution)/shard_map/ppermute | solution.py:33
  110.4 16.8 %collective-permute-start.21 = (bf16[2,64,512]{2,1,0:T(8,128)(2,1)S(1)}, bf16[2,64,512]{2,1,0:T(8,128)(2,1)S(1)}, u32[]{:S(2)}, u32[]{:S(2)}) collective-permute-start(bf16[2,64,512]{2,1,0:T(8,128)(2,1)S(1)} %get-tuple-element.50), channel_id=1, source_target_pairs={{0,192},{2,194},{16,208},{18,210},{32,224},{34,226},{48,240},{50,2... | collective-permute-start | bytes 393224 | tf_op jit(solution)/shard_map/ppermute | solution.py:33
  110.4 22.7 %collective-permute-start.29 = (bf16[4,2,64,512]{3,2,1,0:T(8,128)(2,1)S(1)}, bf16[4,2,64,512]{3,2,1,0:T(8,128)(2,1)S(1)}, u32[]{:S(2)}, u32[]{:S(2)}) collective-permute-start(bf16[4,2,64,512]{3,2,1,0:T(8,128)(2,1)S(1)} %pad_maximum_fusion.3.refs_0_), channel_id=1, source_target_pairs={{0,64},{2,66},{16,80},{18,82},{32,96},{34,98},{48,112},{50,114},{1... | collective-permute-start | bytes 1572872 | tf_op jit(solution)/shard_map/ppermute | solution.py:33
  122.3 10.9 %collective-permute-start.30 = (bf16[4,2,64,512]{3,2,1,0:T(8,128)(2,1)S(1)}, bf16[4,2,64,512]{3,2,1,0:T(8,128)(2,1)S(1)}, u32[]{:S(2)}, u32[]{:S(2)}) collective-permute-start(bf16[4,2,64,512]{3,2,1,0:T(8,128)(2,1)S(1)} %pad_maximum_fusion.3.refs_0_), channel_id=1, source_target_pairs={{0,192},{2,194},{16,208},{18,210},{32,224},{34,226},{48,240},{50,2... | collective-permute-start | bytes 1572872 | tf_op jit(solution)/shard_map/ppermute | solution.py:33
  127.3 22.2 %copy-start.3 = (bf16[384,2048]{1,0:T(8,128)(2,1)S(1)}, bf16[384,2048]{1,0:T(8,128)(2,1)}, u32[]{:S(2)}) copy-start(bf16[384,2048]{1,0:T(8,128)(2,1)} %tok.2) | copy-start | bytes 4718596
  127.3 15.1 %collective-permute-start.22 = (bf16[4,2,64,512]{3,2,1,0:T(8,128)(2,1)S(1)}, bf16[4,2,64,512]{3,2,1,0:T(8,128)(2,1)S(1)}, u32[]{:S(2)}, u32[]{:S(2)}) collective-permute-start(bf16[4,2,64,512]{3,2,1,0:T(8,128)(2,1)S(1)} %pad_maximum_fusion.2.refs_0_), channel_id=1, source_target_pairs={{0,32},{2,35},{16,48},{18,51},{32,1},{34,2},{48,17},{50,18},{1,33}... | collective-permute-start | bytes 1572872 | tf_op jit(solution)/shard_map/ppermute | solution.py:49
  128.0 21.5 %collective-permute-start.23 = (bf16[4,2,64,512]{3,2,1,0:T(8,128)(2,1)S(1)}, bf16[4,2,64,512]{3,2,1,0:T(8,128)(2,1)S(1)}, u32[]{:S(2)}, u32[]{:S(2)}) collective-permute-start(bf16[4,2,64,512]{3,2,1,0:T(8,128)(2,1)S(1)} %pad_maximum_fusion.2.refs_0_), channel_id=1, source_target_pairs={{0,16},{2,18},{16,32},{18,34},{32,48},{34,50},{48,1},{50,3},{1,17}... | collective-permute-start | bytes 1572872 | tf_op jit(solution)/shard_map/ppermute | solution.py:41
  129.2 20.3 %collective-permute-start.24 = (bf16[4,2,64,512]{3,2,1,0:T(8,128)(2,1)S(1)}, bf16[4,2,64,512]{3,2,1,0:T(8,128)(2,1)S(1)}, u32[]{:S(2)}, u32[]{:S(2)}) collective-permute-start(bf16[4,2,64,512]{3,2,1,0:T(8,128)(2,1)S(1)} %pad_maximum_fusion.2.refs_0_), channel_id=1, source_target_pairs={{0,49},{2,51},{16,0},{18,2},{32,16},{34,18},{48,32},{50,34},{1,48}... | collective-permute-start | bytes 1572872 | tf_op jit(solution)/shard_map/ppermute | solution.py:41
  134.8 17.9 %collective-permute-start.32 = (f32[256,384]{1,0:T(8,128)S(1)}, f32[256,384]{1,0:T(8,128)S(1)}, u32[]{:S(2)}, u32[]{:S(2)}) collective-permute-start(f32[256,384]{1,0:T(8,128)S(1)} %get-tuple-element.38), channel_id=1, source_target_pairs={{0,2},{2,0},{16,18},{18,16},{32,34},{34,32},{48,50},{50,48},{1,3},... | collective-permute-start | bytes 1179656 | tf_op jit(solution)/shard_map/ppermute | solution.py:45
  151.1 1.8 %collective-permute-start.31 = (f32[256,384]{1,0:T(8,128)S(1)}, f32[256,384]{1,0:T(8,128)S(1)}, u32[]{:S(2)}, u32[]{:S(2)}) collective-permute-start(f32[256,384]{1,0:T(8,128)S(1)} %get-tuple-element.37), channel_id=1, source_target_pairs={{0,2},{2,0},{16,18},{18,16},{32,34},{34,32},{48,50},{50,48},{1,3},... | collective-permute-start | bytes 1179656 | tf_op jit(solution)/shard_map/ppermute | solution.py:45
  151.9 5.7 %copy-start.5 = (s32[384]{0:T(512)S(1)}, s32[384]{0:T(512)}, u32[]{:S(2)}) copy-start(s32[384]{0:T(512)} %param.15) | copy-start | bytes 4612
  153.2 7.4 %collective-permute-start.33 = (s16[144,384]{1,0:T(8,128)(2,1)S(1)}, s16[144,384]{1,0:T(8,128)(2,1)S(1)}, u32[]{:S(2)}, u32[]{:S(2)}) collective-permute-start(s16[144,384]{1,0:T(8,128)(2,1)S(1)} %get-tuple-element.40), channel_id=1, source_target_pairs={{0,8},{2,10},{16,24},{18,26},{32,40},{34,42},{48,56},{50,58},{1,9}... | collective-permute-start | bytes 331784 | tf_op jit(solution)/shard_map/ppermute | solution.py:37
  154.1 8.3 %collective-permute-start.34 = (s16[144,384]{1,0:T(8,128)(2,1)S(1)}, s16[144,384]{1,0:T(8,128)(2,1)S(1)}, u32[]{:S(2)}, u32[]{:S(2)}) collective-permute-start(s16[144,384]{1,0:T(8,128)(2,1)S(1)} %get-tuple-element.41), channel_id=1, source_target_pairs={{0,4},{2,6},{16,20},{18,22},{32,36},{34,38},{48,52},{50,54},{1,5},... | collective-permute-start | bytes 331784 | tf_op jit(solution)/shard_map/ppermute | solution.py:37
  157.6 5.6 %collective-permute-start.35 = (s16[144,384]{1,0:T(8,128)(2,1)S(1)}, s16[144,384]{1,0:T(8,128)(2,1)S(1)}, u32[]{:S(2)}, u32[]{:S(2)}) collective-permute-start(s16[144,384]{1,0:T(8,128)(2,1)S(1)} %get-tuple-element.42), channel_id=1, source_target_pairs={{0,12},{2,14},{16,28},{18,30},{32,44},{34,46},{48,60},{50,62},{1,1... | collective-permute-start | bytes 331784 | tf_op jit(solution)/shard_map/ppermute | solution.py:37
